TPU v7x, 32 devices: a whole 2x2x4 slice. The times are simulated.
32 devices in a mesh: seq: 8 (over z, y), tp: 4 (over x, core).
Axes of the slice: x: 2, y: 2, z: 4, core: 2. Of those that a mesh axis runs over, the one named last changes fastest.
Arguments:
- queries: bfloat16 [1024, 4096], P('seq', 'tp'), may hold values from -128 to 128
- keys: bfloat16 [1024, 4096], P('seq', 'tp'), may hold values from -6 to 6
- values: bfloat16 [1024, 4096], P('seq', 'tp'), may hold values from -18 to 18
- residual_in: bfloat16 [1024, 4096], P('seq', 'tp'), may hold values from -6 to 6
- norm_gain: float32 [4096], replicated, may hold values from 0.1 to 1.9
- routing: int32 [8, 1], replicated, may hold values from 0 to 3; in each aligned block of 8 rows (0 to 7, 8 to 15, ...) at most 4 rows name the same one
- gate_weight: bfloat16 [8, 4096, 512], P('seq', None, 'tp'), may hold values from -0.09375 to 0.09375
- up_weight: bfloat16 [8, 4096, 512], P('seq', None, 'tp'), may hold values from -0.09375 to 0.09375
- down_weight: bfloat16 [8, 512, 4096], P('seq', None, 'tp'), may hold values from -0.1875 to 0.1875
Outputs:
- mixed: bfloat16 [1024, 4096], P('seq', 'tp')
Inputs may be any that keep to these rules, and one draw needn't show every extreme that they name: `routing`: every expert is named by some block; no expert by more than 4 blocks, and one by exactly 4.
All inputs are finite; a program needn't handle non-finite values.
Results may differ from a plain program's by a relative error of at most 0.006.
Values may be sent and summed in bfloat16 or wider, within the bound.
A program may use at most 64 MiB of HBM per device.

v0:
```python
import math

import jax
import jax.numpy as jnp
from jax import lax
from jax.experimental import pallas as pl
from jax.experimental.pallas import tpu as pltpu
from jax.sharding import PartitionSpec as P

HEAD_DIM = 128
BLOCK = 128
WINDOW = 512


epsilon = 1e-05
masked_score = -1e30


def shifted(block, axis, distance):
    devices = range(lax.axis_size(axis))
    route = [(i - distance, i) for i in devices if i - distance in devices]
    return lax.ppermute(block, axis, route)


def local_general(
    queries, keys, values, residual_in, norm_gain, routing, gate_weight, up_weight, down_weight
):
    seq_count = lax.axis_size("seq")
    seq_place = lax.axis_index("seq")
    tok_rows = queries.shape[0]
    feat_width = queries.shape[1]
    head_count = feat_width // HEAD_DIM
    prior_count = (WINDOW - 1) // tok_rows + 1
    earlier_keys = []
    earlier_values = []
    for distance in range(1, prior_count + 1):
        moved_keys, moved_values = shifted((keys, values), "seq", distance)
        earlier_keys.insert(0, moved_keys)
        earlier_values.insert(0, moved_values)
    key_all = jnp.concatenate(earlier_keys + [keys], axis=0).reshape(-1, head_count, HEAD_DIM)
    value_all = jnp.concatenate(earlier_values + [values], axis=0).reshape(-1, head_count, HEAD_DIM)
    query_heads = queries.reshape(tok_rows, head_count, HEAD_DIM)
    query_pos = seq_place * tok_rows + jnp.arange(tok_rows, dtype=jnp.int32)
    key_pos = (
        seq_place * tok_rows
        - prior_count * tok_rows
        + jnp.arange((prior_count + 1) * tok_rows, dtype=jnp.int32)
    )
    visible = (
        (key_pos[None, :] >= 0)
        & (key_pos[None, :] <= query_pos[:, None])
        & (key_pos[None, :] > query_pos[:, None] - WINDOW)
    )
    scores = jnp.einsum(
        "qhd,khd->hqk", query_heads, key_all, preferred_element_type=jnp.float32
    ) * (1.0 / math.sqrt(HEAD_DIM))
    scores = jnp.where(visible[None], scores, masked_score)
    top_score = jnp.max(scores, axis=2, keepdims=True)
    expo = jnp.exp(scores - top_score)
    weights_soft = (expo / jnp.sum(expo, axis=2, keepdims=True)).astype(jnp.bfloat16)
    attended = jnp.einsum(
        "hqk,khd->qhd", weights_soft, value_all, preferred_element_type=jnp.float32
    ).reshape(tok_rows, feat_width)
    stream = (residual_in.astype(jnp.float32) + attended).astype(jnp.bfloat16)
    send_width = stream.shape[1]
    blocks_dev = tok_rows // BLOCK
    piece_rows = BLOCK // seq_count
    spread_in = stream.reshape(blocks_dev, seq_count, piece_rows, send_width)
    spread_out = lax.all_to_all(spread_in, "seq", split_axis=1, concat_axis=0, tiled=True)
    block_count = blocks_dev * seq_count
    spread_rows = spread_out.reshape(block_count, piece_rows, send_width)
    expert_ids = routing[:, 0]
    expert_count = seq_count // 2
    most_blocks = min(2 * block_count // expert_count, block_count - expert_count + 1)
    order_index = jnp.arange(block_count, dtype=jnp.int32)
    same_expert = expert_ids[None, :] == expert_ids[:, None]
    rank_of = jnp.sum(same_expert & (order_index[None, :] < order_index[:, None]), axis=1)
    expert_range = jnp.arange(expert_count, dtype=jnp.int32)
    slot_range = jnp.arange(most_blocks, dtype=jnp.int32)
    selector = (
        (expert_ids[None, None, :] == expert_range[:, None, None])
        & (rank_of[None, None, :] == slot_range[None, :, None])
    ).astype(jnp.bfloat16)
    picked = jnp.einsum(
        "erb,bqf->erqf", selector, spread_rows, preferred_element_type=jnp.float32
    ).astype(jnp.bfloat16)
    outgoing = jnp.broadcast_to(
        picked[:, None], (expert_count, 2, most_blocks, piece_rows, send_width)
    )
    outgoing = outgoing.reshape(seq_count, most_blocks, piece_rows, send_width)
    features_full = lax.all_gather(
        lax.all_to_all(outgoing, "seq", split_axis=0, concat_axis=0, tiled=True),
        "tp",
        axis=3,
        tiled=True,
    )
    source_count = features_full.shape[0]
    slot_count = features_full.shape[1]
    stream_f32 = features_full.astype(jnp.float32)
    mean_square = jnp.mean(stream_f32 * stream_f32, axis=3, keepdims=True)
    normed = (stream_f32 * lax.rsqrt(mean_square + epsilon) * norm_gain).astype(jnp.bfloat16)
    normed = normed.reshape(-1, normed.shape[3])
    gate_val = jnp.dot(normed, gate_weight[0], preferred_element_type=jnp.float32)
    up_val = jnp.dot(normed, up_weight[0], preferred_element_type=jnp.float32)
    hidden = (jax.nn.silu(gate_val) * up_val).astype(jnp.bfloat16)
    hidden_half = lax.all_gather(hidden, "tp", axis=1, tiled=True)
    partial_value = jnp.dot(hidden_half, down_weight[0], preferred_element_type=jnp.float32).astype(
        jnp.bfloat16
    )
    partial_value = partial_value.reshape(source_count, slot_count, piece_rows, feat_width)
    returned = lax.all_to_all(partial_value, "seq", split_axis=0, concat_axis=0, tiled=True)
    returned = returned.reshape(expert_count, 2, most_blocks, piece_rows * feat_width)
    combined = jnp.einsum("erb,epry->pby", selector, returned, preferred_element_type=jnp.float32)
    residual_rows = spread_rows
    residual_rows = residual_rows.reshape(block_count, piece_rows * feat_width).astype(jnp.float32)
    finished = (residual_rows + combined[0] + combined[1]).astype(jnp.bfloat16)
    finished = finished.reshape(seq_count, blocks_dev, piece_rows, feat_width)
    restored = lax.all_to_all(finished, "seq", split_axis=0, concat_axis=2, tiled=True)
    return restored.reshape(tok_rows, feat_width)


BF16 = jnp.bfloat16
F32 = jnp.float32


def remote(src, dst, send_sem, recv_sem, device):
    return pltpu.make_async_remote_copy(
        src_ref=src,
        dst_ref=dst,
        send_sem=send_sem,
        recv_sem=recv_sem,
        device_id=device,
        device_id_type=pl.DeviceIdType.MESH,
    )


def layer_kernel(planes, most, arguments, out_ref, scratch):
    (
        routing_ref, q_ref, k_ref, v_ref, r_ref, gain_ref, gate_ref, up_ref, down_ref
    ) = arguments
    (
        q_buf,
        r_buf,
        kv_buf,
        line,
        end_out,
        end_in,
        x_buf,
        w_buf,
        acc_buf,
        square_buf,
        hid_buf,
        down_buf,
        mix,
        end_up,
        end_dn,
        up_out,
        up_in,
        dn_out,
        dn_in,
        fin_buf,
        pair_s,
        pair_r,
        local_s,
        kvline_s,
        kvline_r,
        line_s,
        line_r,
        end_s,
        end_r,
        feat_s,
        feat_r,
        hid_s,
        hid_r,
        ret_s,
        ret_r,
        edge_s,
        edge_r,
        last_s,
        last_r,
    ) = scratch
    rows = q_ref.shape[0]
    half = q_ref.shape[1] // 2
    heads = half // HEAD_DIM
    blocks = 2 * planes
    me = lax.axis_index("seq")
    t = lax.axis_index("tp")
    z = me // 2
    y = me % 2
    yo = 1 - y
    mate = 2 * z + yo
    tc = t + 1 - 2 * (t % 2)
    tx = t + 2 - 4 * (t // 2)
    txc = tx + 1 - 2 * (tx % 2)
    dev_y, dev_c, dev_x = (mate, t), (me, tc), (me, tx)
    dev_up, dev_dn = (me + 2, t), (me - 2, t)
    has_up, has_dn = z < planes - 1, z > 0
    unsent = []

    barrier = pltpu.get_barrier_semaphore()

    def greet(device):
        pl.semaphore_signal(
            barrier, inc=1, device_id=device, device_id_type=pl.DeviceIdType.MESH
        )

    for device in (dev_y, dev_c, dev_x):
        greet(device)
    pl.when(has_up)(lambda: greet(dev_up))
    pl.when(has_dn)(lambda: greet(dev_dn))

    def cols(which, h):
        return pl.ds(pl.multiple_of(which * half + h * HEAD_DIM, HEAD_DIM), HEAD_DIM)

    def wide(which):
        return pl.ds(pl.multiple_of(which * half, half), half)

    stay = []
    for h in range(heads):
        stay.append((k_ref.at[:, cols(y, h)], kv_buf.at[0, h, 0, y]))
        stay.append((v_ref.at[:, cols(y, h)], kv_buf.at[0, h, 1, y]))
    stay.append((q_ref.at[:, wide(y)], q_buf.at[y]))
    stay.append((r_ref.at[:, wide(y)], r_buf.at[y]))
    stay.append((gate_ref.at[0], w_buf.at[:, pl.ds(0, gate_ref.shape[2])]))
    stay.append((up_ref.at[0], w_buf.at[:, pl.ds(gate_ref.shape[2], gate_ref.shape[2])]))
    stay.append((down_ref.at[0, :, wide(y)], down_buf.at[y]))
    stay = [pltpu.make_async_copy(a, b, local_s.at[i]) for i, (a, b) in enumerate(stay)]
    for copy in stay:
        copy.start()

    expert = [routing_ref[b] for b in range(blocks)]
    slot = []
    for b in range(blocks):
        count = jnp.int32(0)
        for j in range(b):
            count = count + jnp.where(expert[j] == expert[b], 1, 0)
        slot.append(jnp.minimum(count, most - 1))

    def listing(which):
        found = []
        for r in range(most):
            index = jnp.int32(0)
            for b in range(blocks):
                index = jnp.where((expert[b] == which) & (slot[b] == r), b, index)
            found.append(index)
        return found

    chosen = listing(z)
    at_edge = (z == 0) | (z == planes - 1)
    by_edge = (z == 1) | (z == planes - 2)
    chosen_edge = listing(jnp.where(z == 1, 0, planes - 1))
    dev_edge = (jnp.where(z == 1, me - 2, me + 2), t)
    line_up, line_dn = z < planes - 2, z > 1

    for dist in (1, 2):

        @pl.when(z < dist)
        def _():
            kv_buf[dist] = jnp.zeros(kv_buf.shape[1:], kv_buf.dtype)

    pl.semaphore_wait(
        barrier, 3 + jnp.where(has_up, 1, 0) + jnp.where(has_dn, 1, 0)
    )

    def pair_copy(i, src, dst):
        return remote(src, dst, pair_s.at[i], pair_r.at[i], dev_y)

    swap, landed = [], []
    for h in range(heads):
        for n, ref in enumerate((k_ref, v_ref)):
            i = len(swap)
            swap.append(pair_copy(i, ref.at[:, cols(yo, h)], kv_buf.at[0, h, n, y]))
            landed.append(pair_copy(i, kv_buf.at[0, h, n, yo], kv_buf.at[0, h, n, yo]))
    for ref, buf in ((q_ref, q_buf), (r_ref, r_buf)):
        i = len(swap)
        swap.append(pair_copy(i, ref.at[:, wide(yo)], buf.at[y]))
        landed.append(pair_copy(i, buf.at[yo], buf.at[yo]))
    i = len(swap)
    swap.append(pair_copy(i, down_ref.at[0, :, wide(yo)], down_buf.at[y + 2]))
    landed.append(pair_copy(i, down_buf.at[yo + 2], down_buf.at[yo + 2]))
    for copy in swap:
        copy.start()
        unsent.append((None, copy))

    def kv_copy(dist, h):
        return remote(
            kv_buf.at[dist, h],
            kv_buf.at[dist + 1, h],
            kvline_s.at[dist, h],
            kvline_r.at[dist, h],
            dev_up,
        )

    def kv_own(h):
        for i in (2 * h, 2 * h + 1):
            stay[i].wait()
            landed[i].wait_recv()
        pl.when(has_up)(lambda: kv_copy(0, h).start())
        unsent.append((has_up, kv_copy(0, h)))

    def kv_relay(h):
        pl.when(has_dn)(lambda: kv_copy(0, h).wait_recv())
        pl.when(has_dn & has_up)(lambda: kv_copy(1, h).start())
        unsent.append((has_dn & has_up, kv_copy(1, h)))

    def line_copy(way, plane, h):
        return remote(
            line[h].at[plane],
            line[h].at[plane],
            line_s.at[way, plane, h],
            line_r.at[way, plane, h],
            dev_up if way == 0 else dev_dn,
        )

    row_at = lax.broadcasted_iota(jnp.int32, (rows, rows), 0)
    col_at = lax.broadcasted_iota(jnp.int32, (rows, rows), 1)
    behind = [jnp.where(z >= dist, 0.0, masked_score).astype(F32) for dist in range(3)]

    def attend(h):
        pl.when(z > 1)(lambda: kv_copy(1, h).wait_recv())
        at = pl.ds(h * HEAD_DIM, HEAD_DIM)
        count = WINDOW // rows
        for n in range(2):
            query = q_buf[n, :, at]
            places = []
            for back in range(count + 1):
                dist = (back - n + 1) // 2
                places.append((dist, (n - back) % 2))
            parts = []
            for back, (dist, block) in enumerate(places):
                part = lax.dot_general(
                    query,
                    kv_buf[dist, h, 0, block],
                    (((1,), (1,)), ((), ())),
                    preferred_element_type=F32,
                )
                if back == 0:
                    part = jnp.where(col_at <= row_at, part, masked_score)
                if back == count:
                    part = jnp.where(col_at > row_at, part, masked_score)
                if dist > 0:
                    part = part + behind[dist]
                parts.append(part)
            top = parts[0]
            for part in parts[1:]:
                top = jnp.maximum(top, part)
            top = jnp.max(top, axis=1, keepdims=True)
            parts = [jnp.exp((part - top) * (1.0 / math.sqrt(HEAD_DIM))) for part in parts]
            total = parts[0]
            for part in parts[1:]:
                total = total + part
            share = 1.0 / jnp.sum(total, axis=1, keepdims=True)
            attended = jnp.dot(
                jnp.concatenate([(part * share).astype(BF16) for part in parts], axis=1),
                jnp.concatenate([kv_buf[dist, h, 1, block] for dist, block in places], axis=0),
                preferred_element_type=F32,
            )
            line[h][z, n] = (r_buf[n, :, at].astype(F32) + attended).astype(BF16)
        pl.when(line_up)(lambda: line_copy(0, z, h).start())
        pl.when(line_dn)(lambda: line_copy(1, z, h).start())
        unsent.append((line_up, line_copy(0, z, h)))
        unsent.append((line_dn, line_copy(1, z, h)))

    def end_copy(h):
        return remote(end_out[h], end_in[h], end_s.at[h], end_r.at[h], dev_edge)

    def pick(flag, a, b):
        mask = jnp.full(a.shape, flag.astype(jnp.int32), jnp.int32) > 0
        return jnp.where(mask, a.astype(F32), b.astype(F32)).astype(BF16)

    def spread(h):
        for step in range(1, planes):
            below, above = z - step, z + step
            from_below = (below >= 0) & (z < planes - 1)
            from_above = (above < planes) & (z > 0)

            @pl.when(from_below)
            def _():
                line_copy(0, below, h).wait_recv()
                pl.when(line_up)(lambda: line_copy(0, below, h).start())

            @pl.when(from_above)
            def _():
                line_copy(1, above, h).wait_recv()
                pl.when(line_dn)(lambda: line_copy(1, above, h).start())

            unsent.append((from_below & line_up, line_copy(0, below, h)))
            unsent.append((from_above & line_dn, line_copy(1, above, h)))

        @pl.when(by_edge)
        def _():
            for r in range(most):
                end_out[h][r] = line[h][chosen_edge[r] // 2, chosen_edge[r] % 2]
            end_copy(h).start()

        unsent.append((by_edge, end_copy(h)))

        @pl.when(at_edge)
        def _():
            end_copy(h).wait_recv()
            for r in range(most):
                x_buf[y, t, h, pl.ds(r * rows, rows)] = pick(
                    chosen[r] // 2 == z, line[h][z, chosen[r] % 2], end_in[h][r]
                )

        @pl.when(jnp.logical_not(at_edge))
        def _():
            for r in range(most):
                x_buf[y, t, h, pl.ds(r * rows, rows)] = line[h][chosen[r] // 2, chosen[r] % 2]

    def gatherer(buf, sends, recvs, h):
        middle = buf.shape[3] // 2
        low, high, whole = pl.ds(0, middle), pl.ds(middle, middle), pl.ds(0, 2 * middle)

        def piece(i, at, device):
            ref = buf.at[at[0], at[1], h, at[2]]
            return remote(ref, ref, sends.at[i, h], recvs.at[i, h], device)

        def send(i, at, device):
            piece(i, at, device).start()
            unsent.append((None, piece(i, at, device)))

        def take(i, at):
            piece(i, at, dev_c).wait_recv()

        def first():
            send(0, (y, t, low), dev_x)
            send(1, (y, t, high), dev_y)
            send(2, (y, t, high), dev_x)
            send(3, (y, t, low), dev_y)
            send(4, (y, t, whole), dev_c)

        def second():
            take(0, (y, tx, low))
            send(5, (y, tx, low), dev_y)
            send(7, (y, tx, low), dev_c)
            take(1, (yo, t, high))
            send(6, (yo, t, high), dev_x)
            send(8, (yo, t, high), dev_c)
            take(2, (y, tx, high))
            send(9, (y, tx, high), dev_c)
            take(3, (yo, t, low))
            send(10, (yo, t, low), dev_c)

        def third():
            take(5, (yo, tx, low))
            send(11, (yo, tx, low), dev_c)
            take(6, (yo, tx, high))
            send(12, (yo, tx, high), dev_c)

        def near():
            take(4, (y, tc, whole))
            take(7, (y, txc, low))
            take(9, (y, txc, high))
            take(8, (yo, tc, high))
            take(10, (yo, tc, low))

        def far():
            take(11, (yo, txc, low))
            take(12, (yo, txc, high))

        return first, second, third, near, far

    def expert_parts(parts, pair):
        left, right = [], []
        square = square_buf[...]
        for py, pt in parts:
            for h in (2 * pair, 2 * pair + 1):
                start = pl.multiple_of((2 * pt + py) * half + h * HEAD_DIM, HEAD_DIM)
                x = x_buf[py, pt, h].astype(F32)
                square = square + jnp.sum(x * x, axis=1, keepdims=True)
                left.append((x * gain_ref[:, pl.ds(start, HEAD_DIM)]).astype(BF16))
                right.append(w_buf[pl.ds(start, HEAD_DIM), :])
        square_buf[...] = square
        acc_buf[...] += jnp.dot(
            jnp.concatenate(left, axis=1),
            jnp.concatenate(right, axis=0),
            preferred_element_type=F32,
        )

    stages = [gatherer(x_buf, feat_s, feat_r, h) for h in range(heads)]
    most_parts = [(y, t), (y, tc), (y, tx), (yo, t), (y, txc), (yo, tc)]
    rest_parts = [(yo, tx), (yo, txc)]
    for h in range(heads):
        kv_own(h)
    kv_relay(0)
    for i in (2 * heads, 2 * heads + 1):
        stay[i].wait()
        landed[i].wait_recv()
    for turn in range(heads + 3):
        if turn + 1 < heads:
            kv_relay(turn + 1)
        if turn < heads:
            attend(turn)
        if turn == heads:
            acc_buf[...] = jnp.zeros_like(acc_buf)
            square_buf[...] = jnp.zeros_like(square_buf)
            for copy in stay[2 * heads + 2 :]:
                copy.wait()
        if 0 <= turn - 1 < heads:
            spread(turn - 1)
            stages[turn - 1][0]()
        if 0 <= turn - 2 < heads:
            stages[turn - 2][1]()
        if 0 <= turn - 3 < heads:
            h = turn - 3
            if h == heads - 1:
                stages[h][3]()
                expert_parts(most_parts, h // 2)
            stages[h][2]()
            if h < heads - 1:
                stages[h][3]()
            stages[h][4]()
            if h == heads - 1:
                expert_parts(rest_parts, h // 2)
            elif h % 2 == 1:
                expert_parts(most_parts + rest_parts, h // 2)
    units = gate_ref.shape[2]
    features = gain_ref.shape[1]
    scale = lax.rsqrt(square_buf[...] * (1.0 / features) + epsilon)
    gate_val = acc_buf[:, pl.ds(0, units)] * scale
    up_val = acc_buf[:, pl.ds(units, units)] * scale
    hid_buf[y, t, 0] = (gate_val / (1.0 + jnp.exp(-gate_val)) * up_val).astype(BF16)
    for stage in gatherer(hid_buf, hid_s, hid_r, 0):
        stage()

    chunks = len(mix)
    span = half // chunks
    per = span // HEAD_DIM

    def edge_copy(way, c):
        dst = end_up[c] if way == 0 else end_dn[c]
        return remote(
            mix[c], dst, edge_s.at[way, c], edge_r.at[way, c], dev_up if way == 0 else dev_dn
        )

    def ret_copy(way, d, c):
        out, arrived = (up_out, up_in) if way == 0 else (dn_out, dn_in)
        return remote(
            out.at[c, d],
            arrived.at[c, d],
            ret_s.at[way, d, c],
            ret_r.at[way, d, c],
            dev_up if way == 0 else dev_dn,
        )

    landed[2 * heads + 2].wait_recv()
    hidden = [
        jnp.concatenate([hid_buf[h, i, 0] for i in range(hid_buf.shape[1])], axis=1)
        for h in range(2)
    ]
    for c in range(chunks):
        total = jnp.concatenate(
            [x_buf[y, t, c * per + i] for i in range(per)], axis=1
        ).astype(F32)
        for h in range(2):
            weight = down_buf[h + 2 * ((y + h) % 2), :, pl.ds(c * span, span)]
            branch = jnp.dot(hidden[h], weight, preferred_element_type=F32).astype(BF16)
            total = total + branch.astype(F32)
        mix[c][...] = total.astype(BF16).reshape(most, rows, span)
        pl.when(z == 0)(lambda: edge_copy(0, c).start())
        pl.when(z == planes - 1)(lambda: edge_copy(1, c).start())
        unsent.append((z == 0, edge_copy(0, c)))
        unsent.append((z == planes - 1, edge_copy(1, c)))

    def relay(c, close):
        if close:
            pl.when(z == 1)(lambda: edge_copy(0, c).wait_recv())
            pl.when(z == planes - 2)(lambda: edge_copy(1, c).wait_recv())
        for step in range(planes - 1):
            for way, d in ((0, planes - 1 - step), (1, step)):
                passes = (z < d) & (z > 0) if way == 0 else (z > d) & (z < planes - 1)
                near = z == 1 if way == 0 else z == planes - 2
                end = end_up[c] if way == 0 else end_dn[c]
                out, arrived = (up_out, up_in) if way == 0 else (dn_out, dn_in)
                here = passes & near if close else passes & jnp.logical_not(near)

                @pl.when(here)
                def _():
                    if not close:
                        ret_copy(way, d, c).wait_recv()
                    for n in range(2):
                        b = 2 * d + n
                        other = end[slot[b]] if close else arrived[c, d, n]
                        out[c, d, n] = pick(expert[b] == z, mix[c][slot[b]], other)
                    ret_copy(way, d, c).start()

                unsent.append((here, ret_copy(way, d, c)))

    def finish(which, c):
        return pl.ds(pl.multiple_of(which * half + c * span, span), span)

    def last_copy(c):
        return remote(
            fin_buf.at[c, yo], out_ref.at[:, finish(y, c)], last_s.at[c], last_r.at[c], dev_y
        )

    def arrive(c):
        for d in range(planes):

            @pl.when(z == d)
            def _():
                if d > 1:
                    ret_copy(0, d, c).wait_recv()
                if d < planes - 2:
                    ret_copy(1, d, c).wait_recv()
                for n in range(2):
                    b = 2 * d + n
                    value = mix[c][slot[b]]
                    if d > 0:
                        value = pick(
                            expert[b] < z, up_in[c, d, n] if d > 1 else end_up[c][slot[b]], value
                        )
                    if d < planes - 1:
                        value = pick(
                            expert[b] > z,
                            dn_in[c, d, n] if d < planes - 2 else end_dn[c][slot[b]],
                            value,
                        )
                    fin_buf[c, n] = value

        last_copy(c).start()
        unsent.append((None, last_copy(c)))
        out_ref[:, finish(y, c)] = fin_buf[c, y]
    relay(0, True)
    for c in range(chunks):
        if c + 1 < chunks:
            relay(c + 1, True)
        relay(c, False)
        if c > 0:
            arrive(c - 1)
    arrive(chunks - 1)
    for c in range(chunks):
        mine = out_ref.at[:, finish(yo, c)]
        remote(mine, mine, last_s.at[c], last_r.at[c], dev_y).wait_recv()
    for flag, copy in unsent:
        if flag is None:
            copy.wait_send()
        else:
            pl.when(flag)(lambda: copy.wait_send())


def local(
    queries, keys, values, residual_in, norm_gain, routing, gate_weight, up_weight, down_weight
):
    seq_count = lax.axis_size("seq")
    tp_count = lax.axis_size("tp")
    rows, width = queries.shape
    units = gate_weight.shape[2]
    planes = seq_count // 2
    fits = (
        tp_count == 4
        and seq_count % 2 == 0
        and 4 <= planes <= 8
        and rows == BLOCK
        and WINDOW == 4 * rows
        and units == 128
        and width % (8 * HEAD_DIM) == 0
    )
    if not fits:
        return local_general(
            queries,
            keys,
            values,
            residual_in,
            norm_gain,
            routing,
            gate_weight,
            up_weight,
            down_weight,
        )
    half = width // 2
    heads = half // HEAD_DIM
    most = min(2 * seq_count // planes, seq_count - planes + 1)
    chunks = 4
    span = half // chunks
    vmem = pl.BlockSpec(memory_space=pltpu.VMEM)
    anywhere = pl.BlockSpec(memory_space=pltpu.MemorySpace.HBM)
    dma = pltpu.SemaphoreType.DMA

    def room(*shape, kind=BF16):
        return pltpu.VMEM(shape, kind)

    scratch = (
        room(2, rows, half),
        room(2, rows, half),
        room(3, heads, 2, 2, rows, HEAD_DIM),
        [room(planes, 2, rows, HEAD_DIM) for _ in range(heads)],
        [room(most, rows, HEAD_DIM) for _ in range(heads)],
        [room(most, rows, HEAD_DIM) for _ in range(heads)],
        room(2, tp_count, heads, most * rows, HEAD_DIM),
        room(norm_gain.shape[0], 2 * units),
        room(most * rows, 2 * units, kind=F32),
        room(most * rows, 1, kind=F32),
        room(2, tp_count, 1, most * rows, units),
        room(4, down_weight.shape[1], half),
        [room(most, rows, span) for _ in range(chunks)],
        [room(most, rows, span) for _ in range(chunks)],
        [room(most, rows, span) for _ in range(chunks)],
        room(chunks, planes, 2, rows, span),
        room(chunks, planes, 2, rows, span),
        room(chunks, planes, 2, rows, span),
        room(chunks, planes, 2, rows, span),
        room(chunks, 2, rows, span),
        dma((2 * heads + 3,)),
        dma((2 * heads + 3,)),
        dma((2 * heads + 5,)),
        dma((2, heads)),
        dma((2, heads)),
        dma((2, planes, heads)),
        dma((2, planes, heads)),
        dma((heads,)),
        dma((heads,)),
        dma((13, heads)),
        dma((13, heads)),
        dma((13, 1)),
        dma((13, 1)),
        dma((2, planes, chunks)),
        dma((2, planes, chunks)),
        dma((2, chunks)),
        dma((2, chunks)),
        dma((chunks,)),
        dma((chunks,)),
    )
    flat, tree = jax.tree.flatten(scratch, is_leaf=lambda leaf: not isinstance(leaf, (list, tuple)))

    def kernel(*refs):
        layer_kernel(planes, most, refs[:9], refs[9], jax.tree.unflatten(tree, refs[10:]))

    return pl.pallas_call(
        kernel,
        name="layer",
        out_shape=jax.ShapeDtypeStruct((rows, width), BF16),
        in_specs=[pl.BlockSpec(memory_space=pltpu.SMEM)]
        + [anywhere] * 4
        + [vmem]
        + [anywhere] * 3,
        out_specs=vmem,
        scratch_shapes=flat,
        compiler_params=pltpu.CompilerParams(
            collective_id=0, has_side_effects=True, vmem_limit_bytes=67043328
        ),
    )(
        routing.reshape(-1),
        queries,
        keys,
        values,
        residual_in,
        norm_gain.reshape(1, -1),
        gate_weight,
        up_weight,
        down_weight,
    )


def solution(mesh):
    in_specs = (
        P("seq", "tp"),
        P("seq", "tp"),
        P("seq", "tp"),
        P("seq", "tp"),
        P(),
        P(),
        P("seq", None, "tp"),
        P("seq", None, "tp"),
        P("seq", None, "tp"),
    )
    out_specs = P("seq", "tp")
    return jax.shard_map(local, mesh=mesh, in_specs=in_specs, out_specs=out_specs, check_vma=False)
```

profile of v0, /device:TPU:1, one launch (start us, length us, event | category | flops | bytes accessed | tf_op | source)
XLA Modules:
  0.0 101.2 jit_solution(9180506516127105578)
XLA Ops:
  0.0 99.5 %layer.1 = bf16[128,1024]{1,0:T(8,128)(2,1)} custom-call(s32[8]{0:T(128)} %bitcast.3, bf16[128,1024]{1,0:T(8,128)(2,1)} %refs_1_.1, bf16[128,1024]{1,0:T(8,128)(2,1)} %refs_2_.1, bf16[128,1024]{1,0:T(8,128)(2,1)} %refs_3_.1, bf16[128,1024]{1,0:T(8,128)(2,1)} %refs_4_.1, f32[1,4096]{1,0:T(1,128)} %bitcast.2, bf16[1,4096,128]{2,1,0:T(8,128)(2,1)} %refs_6_.1, ...), custom_call_target="tpu_custom_call" | custom-call | tf_op jit(solution)/shard_map/layer/pallas_call | solution.py:730
  99.5 1.7 %copy.11 = bf16[128,1024]{1,0:T(8,128)(2,1)} copy(bf16[128,1024]{1,0:T(8,128)(2,1)} %layer.1) | data formatting | bytes 524288
where the time goes:
time: 103 us; the launch traced here: 101 us
  Pallas kernels  99.5 us (97%)
  local copies, waits for them, and re-layouts  1.67 us (2%)
    pallas_call x1, Pallas kernels, local(): pl.pallas_call(kernel, name='layer', out_shape=jax.ShapeDtypeStruct((rows...  99.5 us

commit v1 on v0

v1 whole, which is shorter than its diff:
```python
import contextlib
import math

import jax
import jax.numpy as jnp
from jax import lax
from jax.experimental import pallas as pl
from jax.experimental.pallas import tpu as pltpu
from jax.sharding import PartitionSpec as P

HEAD_DIM = 128
BLOCK = 128
WINDOW = 512


epsilon = 1e-05
masked_score = -1e30


def shifted(block, axis, distance):
    devices = range(lax.axis_size(axis))
    route = [(i - distance, i) for i in devices if i - distance in devices]
    return lax.ppermute(block, axis, route)


def local_general(
    queries, keys, values, residual_in, norm_gain, routing, gate_weight, up_weight, down_weight
):
    seq_count = lax.axis_size("seq")
    seq_place = lax.axis_index("seq")
    tok_rows = queries.shape[0]
    feat_width = queries.shape[1]
    head_count = feat_width // HEAD_DIM
    prior_count = (WINDOW - 1) // tok_rows + 1
    earlier_keys = []
    earlier_values = []
    for distance in range(1, prior_count + 1):
        moved_keys, moved_values = shifted((keys, values), "seq", distance)
        earlier_keys.insert(0, moved_keys)
        earlier_values.insert(0, moved_values)
    key_all = jnp.concatenate(earlier_keys + [keys], axis=0).reshape(-1, head_count, HEAD_DIM)
    value_all = jnp.concatenate(earlier_values + [values], axis=0).reshape(-1, head_count, HEAD_DIM)
    query_heads = queries.reshape(tok_rows, head_count, HEAD_DIM)
    query_pos = seq_place * tok_rows + jnp.arange(tok_rows, dtype=jnp.int32)
    key_pos = (
        seq_place * tok_rows
        - prior_count * tok_rows
        + jnp.arange((prior_count + 1) * tok_rows, dtype=jnp.int32)
    )
    visible = (
        (key_pos[None, :] >= 0)
        & (key_pos[None, :] <= query_pos[:, None])
        & (key_pos[None, :] > query_pos[:, None] - WINDOW)
    )
    scores = jnp.einsum(
        "qhd,khd->hqk", query_heads, key_all, preferred_element_type=jnp.float32
    ) * (1.0 / math.sqrt(HEAD_DIM))
    scores = jnp.where(visible[None], scores, masked_score)
    top_score = jnp.max(scores, axis=2, keepdims=True)
    expo = jnp.exp(scores - top_score)
    weights_soft = (expo / jnp.sum(expo, axis=2, keepdims=True)).astype(jnp.bfloat16)
    attended = jnp.einsum(
        "hqk,khd->qhd", weights_soft, value_all, preferred_element_type=jnp.float32
    ).reshape(tok_rows, feat_width)
    stream = (residual_in.astype(jnp.float32) + attended).astype(jnp.bfloat16)
    send_width = stream.shape[1]
    blocks_dev = tok_rows // BLOCK
    piece_rows = BLOCK // seq_count
    spread_in = stream.reshape(blocks_dev, seq_count, piece_rows, send_width)
    spread_out = lax.all_to_all(spread_in, "seq", split_axis=1, concat_axis=0, tiled=True)
    block_count = blocks_dev * seq_count
    spread_rows = spread_out.reshape(block_count, piece_rows, send_width)
    expert_ids = routing[:, 0]
    expert_count = seq_count // 2
    most_blocks = min(2 * block_count // expert_count, block_count - expert_count + 1)
    order_index = jnp.arange(block_count, dtype=jnp.int32)
    same_expert = expert_ids[None, :] == expert_ids[:, None]
    rank_of = jnp.sum(same_expert & (order_index[None, :] < order_index[:, None]), axis=1)
    expert_range = jnp.arange(expert_count, dtype=jnp.int32)
    slot_range = jnp.arange(most_blocks, dtype=jnp.int32)
    selector = (
        (expert_ids[None, None, :] == expert_range[:, None, None])
        & (rank_of[None, None, :] == slot_range[None, :, None])
    ).astype(jnp.bfloat16)
    picked = jnp.einsum(
        "erb,bqf->erqf", selector, spread_rows, preferred_element_type=jnp.float32
    ).astype(jnp.bfloat16)
    outgoing = jnp.broadcast_to(
        picked[:, None], (expert_count, 2, most_blocks, piece_rows, send_width)
    )
    outgoing = outgoing.reshape(seq_count, most_blocks, piece_rows, send_width)
    features_full = lax.all_gather(
        lax.all_to_all(outgoing, "seq", split_axis=0, concat_axis=0, tiled=True),
        "tp",
        axis=3,
        tiled=True,
    )
    source_count = features_full.shape[0]
    slot_count = features_full.shape[1]
    stream_f32 = features_full.astype(jnp.float32)
    mean_square = jnp.mean(stream_f32 * stream_f32, axis=3, keepdims=True)
    normed = (stream_f32 * lax.rsqrt(mean_square + epsilon) * norm_gain).astype(jnp.bfloat16)
    normed = normed.reshape(-1, normed.shape[3])
    gate_val = jnp.dot(normed, gate_weight[0], preferred_element_type=jnp.float32)
    up_val = jnp.dot(normed, up_weight[0], preferred_element_type=jnp.float32)
    hidden = (jax.nn.silu(gate_val) * up_val).astype(jnp.bfloat16)
    hidden_half = lax.all_gather(hidden, "tp", axis=1, tiled=True)
    partial_value = jnp.dot(hidden_half, down_weight[0], preferred_element_type=jnp.float32).astype(
        jnp.bfloat16
    )
    partial_value = partial_value.reshape(source_count, slot_count, piece_rows, feat_width)
    returned = lax.all_to_all(partial_value, "seq", split_axis=0, concat_axis=0, tiled=True)
    returned = returned.reshape(expert_count, 2, most_blocks, piece_rows * feat_width)
    combined = jnp.einsum("erb,epry->pby", selector, returned, preferred_element_type=jnp.float32)
    residual_rows = spread_rows
    residual_rows = residual_rows.reshape(block_count, piece_rows * feat_width).astype(jnp.float32)
    finished = (residual_rows + combined[0] + combined[1]).astype(jnp.bfloat16)
    finished = finished.reshape(seq_count, blocks_dev, piece_rows, feat_width)
    restored = lax.all_to_all(finished, "seq", split_axis=0, concat_axis=2, tiled=True)
    return restored.reshape(tok_rows, feat_width)


BF16 = jnp.bfloat16
F32 = jnp.float32
PLANES = 4
GROUPS = 2
SPAN = 2 * HEAD_DIM
STAY_HEAD = 3


def mark(name):
    return contextlib.nullcontext()


def remote(src, dst, send_sem, recv_sem, device):
    return pltpu.make_async_remote_copy(
        src_ref=src,
        dst_ref=dst,
        send_sem=send_sem,
        recv_sem=recv_sem,
        device_id=device,
        device_id_type=pl.DeviceIdType.MESH,
    )


def size_of(ref):
    return math.prod(ref.shape) * ref.dtype.itemsize


def layer_kernel(most, arguments, out_ref, scratch):
    routing_ref, q_ref, k_ref, v_ref, r_ref, gain_ref, gate_ref, up_ref, down_ref = arguments
    (
        kv_buf,
        qr_buf,
        away,
        line,
        x_buf,
        x_other,
        w_buf,
        d_buf,
        acc_buf,
        square_buf,
        hid_buf,
        b_out,
        b_in,
        part,
        mix,
        end_in,
        up_out,
        up_in,
        dn_out,
        dn_in,
        fin,
        own_s,
        away_s,
        weight_s,
        swap_r,
        kv_r,
        qr_r,
        line_r,
        feat_r,
        weight_r,
        hid_r,
        branch_r,
        end_r,
        ret_r,
        last_r,
        sent,
        plane_sent,
    ) = scratch
    rows = q_ref.shape[0]
    half = q_ref.shape[1] // 2
    heads = half // HEAD_DIM
    units = gate_ref.shape[2]
    features = gain_ref.shape[1]
    core_rows = rows // 2
    group_rows = core_rows // GROUPS
    me = lax.axis_index("seq")
    t = lax.axis_index("tp")
    z = me // 2
    y = me % 2
    x = t // 2
    c = t % 2
    yo, xo, co = 1 - y, 1 - x, 1 - c
    tc = 2 * x + co
    tx = 2 * xo + c
    txc = 2 * xo + co
    mate = 2 * z + yo
    dev_y, dev_yc = (mate, t), (mate, tc)
    dev_x, dev_xc = (me, tx), (me, txc)
    dev_c = (me, tc)
    dev_up, dev_dn = (me + 2, t), (me - 2, t)
    has_up, has_dn = z < PLANES - 1, z > 0

    limit = size_of(w_buf.at[0])
    all_lots = [0]
    plane_lots = [[0] for _ in range(PLANES)]

    def lot_for(lots, ref):
        if lots[-1] + size_of(ref) > limit:
            lots.append(0)
        lots[-1] += size_of(ref)
        return len(lots) - 1

    def push(src, dst, recv_sem, device):
        lot = lot_for(all_lots, src)
        remote(src, dst, sent.at[lot], recv_sem, device).start()

    def push_plane(plane, src, dst, recv_sem, device):
        lot = lot_for(plane_lots[plane], src)
        remote(src, dst, plane_sent.at[lot], recv_sem, device).start()

    def got(ref, recv_sem):
        remote(ref, ref, sent.at[0], recv_sem, dev_y).wait_recv()

    def wait_for(amount, recv_sem):
        got(w_buf.at[0, pl.ds(0, amount // (2 * units))], recv_sem)

    def loaded(ref, sem):
        pltpu.make_async_copy(ref, ref, sem).wait()

    barrier = pltpu.get_barrier_semaphore()

    def greet(device):
        pl.semaphore_signal(
            barrier, inc=1, device_id=device, device_id_type=pl.DeviceIdType.MESH
        )

    for device in (dev_y, dev_yc, dev_c, dev_x, dev_xc):
        greet(device)
    pl.when(has_up)(lambda: greet(dev_up))
    pl.when(has_dn)(lambda: greet(dev_dn))

    def cols(which, h):
        return pl.ds(pl.multiple_of(which * half + h * HEAD_DIM, HEAD_DIM), HEAD_DIM)

    sources = ((k_ref, v_ref), (q_ref, r_ref))

    def place(kind, h, n, block):
        buf = kv_buf if kind == 0 else qr_buf
        return buf.at[0, h, n, block]

    def load_own(kind, h):
        for n, ref in enumerate(sources[kind]):
            pltpu.make_async_copy(
                ref.at[:, cols(y, h)], place(kind, h, n, y), own_s.at[kind, h]
            ).start()

    def load_away(kind, h):
        for n, ref in enumerate(sources[kind]):
            pltpu.make_async_copy(
                ref.at[:, cols(yo, h)], away.at[kind, h, n], away_s.at[kind, h]
            ).start()

    def swap(kind, h):
        loaded(away.at[kind, h], away_s.at[kind, h])
        buf = kv_buf if kind == 0 else qr_buf
        push(away.at[kind, h], buf.at[0, h, :, y], swap_r.at[kind, h], dev_y)

    def own(kind, h):
        buf = kv_buf if kind == 0 else qr_buf
        loaded(buf.at[0, h, :, y], own_s.at[kind, h])
        got(buf.at[0, h, :, yo], swap_r.at[kind, h])

    for kind in range(2):
        for h in range(heads):
            load_away(kind, h)
    for kind in range(2):
        for h in range(heads):
            load_own(kind, h)

    expert = [routing_ref[b] for b in range(2 * PLANES)]
    slot = []
    for b in range(2 * PLANES):
        count = jnp.int32(0)
        for j in range(b):
            count = count + jnp.where(expert[j] == expert[b], 1, 0)
        slot.append(jnp.minimum(count, most - 1))
    chosen = []
    for r in range(most):
        index = jnp.int32(0)
        for b in range(2 * PLANES):
            index = jnp.where((expert[b] == z) & (slot[b] == r), b, index)
        chosen.append(index)

    with mark("barwait"):
        pl.semaphore_wait(barrier, 5 + jnp.where(has_up, 1, 0) + jnp.where(has_dn, 1, 0))

    low_order = ((0, 3), (0, 0), (1, 3), (1, 0), (0, 1), (0, 2), (1, 1), (1, 2))
    high_order = ((0, 0), (1, 0), (0, 1), (1, 1), (0, 3), (0, 2), (1, 2), (1, 3))

    @pl.when(z < 2)
    def _():
        for kind, h in low_order:
            swap(kind, h)

    all_lots[:] = [0]

    @pl.when(z >= 2)
    def _():
        for kind, h in high_order:
            swap(kind, h)

    weights = (
        (gate_ref.at[0], w_buf.at[c]),
        (up_ref.at[0], w_buf.at[2 + c]),
        (down_ref.at[0], d_buf.at[c]),
    )
    for i, (src, dst) in enumerate(weights):
        pltpu.make_async_copy(src, dst, weight_s.at[i]).start()
        push(src, dst, weight_r.at[i], dev_c)

    row_at = lax.broadcasted_iota(jnp.int32, (rows, rows), 0)
    col_at = lax.broadcasted_iota(jnp.int32, (rows, rows), 1)
    below, above, farther = 1, 2, 3

    def attend(here, plane, h):
        side = 0 if plane == here else 1
        keep = {here: 0, here - 1: below, here + 1: above, here - 2: farther}
        reach = WINDOW // rows
        for n in range(2):
            block = 2 * plane + n
            seen = [
                (back, keep[(block - back) // 2], (block - back) % 2)
                for back in range(reach + 1)
                if block >= back
            ]
            query = qr_buf[side, h, 0, n]
            parts = []
            for back, at, odd in seen:
                score = lax.dot_general(
                    query,
                    kv_buf[at, h, 0, odd],
                    (((1,), (1,)), ((), ())),
                    preferred_element_type=F32,
                )
                if back == 0:
                    score = jnp.where(col_at <= row_at, score, masked_score)
                if back == reach:
                    score = jnp.where(col_at > row_at, score, masked_score)
                parts.append(score)
            top = parts[0]
            for score in parts[1:]:
                top = jnp.maximum(top, score)
            top = jnp.max(top, axis=1, keepdims=True)
            parts = [jnp.exp((score - top) * (1.0 / math.sqrt(HEAD_DIM))) for score in parts]
            total = parts[0]
            for score in parts[1:]:
                total = total + score
            share = 1.0 / jnp.sum(total, axis=1, keepdims=True)
            attended = jnp.dot(
                jnp.concatenate([(score * share).astype(BF16) for score in parts], axis=1),
                jnp.concatenate([kv_buf[at, h, 1, odd] for _, at, odd in seen], axis=0),
                preferred_element_type=F32,
            )
            stream = (qr_buf[side, h, 1, n].astype(F32) + attended).astype(BF16)
            line[h][block] = stream.reshape(2, core_rows, HEAD_DIM)

    def device_at(way):
        return dev_up if way > 0 else dev_dn

    def send_kv(here, way, src, dst, h):
        push_plane(here, kv_buf.at[src, h], kv_buf.at[dst, h], kv_r.at[dst, h], device_at(way))

    def got_kv(at, h):
        got(kv_buf.at[at, h], kv_r.at[at, h])

    def send_qr(here, h):
        push_plane(here, qr_buf.at[0, h], qr_buf.at[1, h], qr_r.at[h], dev_dn)

    def got_qr(h):
        got(qr_buf.at[1, h], qr_r.at[h])

    def send_line(here, way, plane, h):
        ref = line[h].at[pl.ds(2 * plane, 2)]
        push_plane(here, ref, ref, line_r.at[plane, h], device_at(way))

    def got_line(plane, h):
        got(line[h].at[pl.ds(2 * plane, 2)], line_r.at[plane, h])

    taken = [set() for _ in range(PLANES)]

    def made(here, plane, h):
        taken[here].add((plane, h))
        with mark(f"attend{plane}_{h}"):
            attend(here, plane, h)
        if here < PLANES - 1:
            send_line(here, 1, plane, h)
        if here > 0:
            send_line(here, -1, plane, h)

    def pass_on(here, way, plane, h):
        with mark(f"pass{plane}_{h}"):
            taken[here].add((plane, h))
            got_line(plane, h)
            send_line(here, way, plane, h)

    def steps_0(step):
        if step == 0:
            for kind, h in low_order:
                with mark(f"own{kind}_{h}"):
                    own(kind, h)
                if kind == 0:
                    send_kv(0, 1, 0, below, h)
                else:
                    made(0, 0, h)

    def steps_1(step):
        def first(h):
            with mark(f"own0_{h}"):
                own(0, h)
            send_kv(1, 1, 0, below, h)

        def home(h):
            with mark(f"own1_{h}"):
                own(1, h)
                got_kv(below, h)
            if h == STAY_HEAD:
                send_kv(1, 1, below, farther, h)
            made(1, 1, h)

        def lower(h):
            with mark(f"lower{h}"):
                got_kv(above, h)
                got_qr(h)
            made(1, 2, h)

        if step == 0:
            first(3)
            first(0)
            home(3)
            first(1)
            home(0)
            pass_on(1, 1, 0, 3)
            first(2)
            lower(0)
            pass_on(1, 1, 0, 0)
            home(1)
            lower(1)
            pass_on(1, 1, 0, 1)
            home(2)
            pass_on(1, 1, 0, 2)
            lower(2)
            pass_on(1, -1, 3, 0)
        if step == 1:
            pass_on(1, -1, 2, 3)
            pass_on(1, -1, 3, 3)
        if step == 2:
            pass_on(1, -1, 3, 1)
        if step == 3:
            pass_on(1, -1, 3, 2)

    def steps_2(step):
        def first(h):
            with mark(f"own0_{h}"):
                own(0, h)
            if h == STAY_HEAD:
                send_kv(2, 1, 0, below, h)
            else:
                send_kv(2, -1, 0, above, h)

        def second(h):
            with mark(f"own1_{h}"):
                own(1, h)
            if h != STAY_HEAD:
                send_qr(2, h)

        def lower(h):
            with mark(f"lower{h}"):
                got_kv(above, h)
                got_kv(below, h)
                got_qr(h)
            made(2, 3, h)

        if step == 0:
            for kind, h in high_order:
                if (kind, h) == (1, 2):
                    with mark("below3"):
                        got_kv(below, 3)
                    send_kv(2, 1, below, farther, 3)
                (second if kind else first)(h)
            lower(0)
            with mark("farther3"):
                got_kv(farther, 3)
            made(2, 2, 3)
            pass_on(2, 1, 1, 3)
            lower(1)
            pass_on(2, 1, 0, 3)
            pass_on(2, 1, 1, 0)
            lower(2)
            pass_on(2, 1, 0, 0)
            pass_on(2, -1, 3, 3)
            pass_on(2, 1, 2, 0)
        if step == 2:
            pass_on(2, 1, 1, 1)
            pass_on(2, 1, 0, 1)
            pass_on(2, 1, 2, 1)
        if step == 3:
            pass_on(2, 1, 1, 2)
            pass_on(2, 1, 0, 2)
            pass_on(2, 1, 2, 2)

    def steps_3(step):
        if step == 0:
            for kind, h in high_order:
                with mark(f"own{kind}_{h}"):
                    own(kind, h)
                if h != STAY_HEAD:
                    if kind == 0:
                        send_kv(3, -1, 0, above, h)
                    else:
                        send_qr(3, h)
            with mark("below3"):
                got_kv(below, 3)
                got_kv(farther, 3)
            made(3, 3, 3)

    def planes(step):
        for plane, steps in enumerate((steps_0, steps_1, steps_2, steps_3)):

            @pl.when(z == plane)
            def _():
                steps(step)

    def collect(h):
        for plane in range(PLANES):

            @pl.when(z == plane)
            def _():
                for other in range(PLANES):
                    if (other, h) not in taken[plane]:
                        taken[plane].add((other, h))
                        got_line(other, h)

    def groups_of(h):
        return [pl.ds(g, 1) for g in range(GROUPS)] if h == order[-1] else [pl.ds(0, GROUPS)]

    def feature_at(h, g):
        return order.index(h) + g.start

    def feature(n, py, pt, h, g, device, src=None):
        ref = x_buf.at[py, pt, h, g]
        push(ref if src is None else src, ref, feat_r.at[lot_of[n], feature_at(h, g)], device)

    lot_of = (0, 0, 1, 2, 0, 3, 3)
    arrivals = (
        (y, tc),
        (y, tx),
        (y, txc),
        (yo, t),
        (yo, tc),
        (yo, tx),
        (yo, txc),
    )

    def take(n, h, g):
        py, pt = arrivals[n]
        got(x_buf.at[py, pt, h, g], feat_r.at[lot_of[n], feature_at(h, g)])

    def first_stage(h):
        for g in groups_of(h):
            for r in range(most):
                at = pl.ds(r * group_rows, group_rows)
                for ref, side in ((x_buf.at[y, t, h], c), (x_other.at[h], co)):
                    block = line[h][chosen[r], side]
                    for i in range(GROUPS):
                        if g.start <= i < g.start + g.size:
                            ref[i, at] = block[i * group_rows : (i + 1) * group_rows]
            other = x_other.at[h, g]
            feature(3, y, t, h, g, dev_y)
            feature(2, y, t, h, g, dev_xc, other)
            feature(1, y, t, h, g, dev_x)
            feature(4, y, t, h, g, dev_yc, other)
            feature(0, y, t, h, g, dev_c, other)

    def second_stage(h, g):
        take(3, h, g)
        feature(5, yo, t, h, g, dev_x)
        take(2, h, g)
        feature(6, y, txc, h, g, dev_y)

    def near(h, g):
        wait_for(3 * size_of(x_buf.at[y, t, h, g]), feat_r.at[0, feature_at(h, g)])

    def far(h, g):
        wait_for(2 * size_of(x_buf.at[y, t, h, g]), feat_r.at[3, feature_at(h, g)])

    def expert_parts(parts, h, g):
        depth = g.size * most * group_rows
        left, right = [], []
        square = square_buf[g].reshape(depth, 1)
        for py, pt in parts:
            start = pl.multiple_of((2 * pt + py) * half + h * HEAD_DIM, HEAD_DIM)
            value = x_buf[py, pt, h, g].reshape(depth, HEAD_DIM).astype(F32)
            square = square + jnp.sum(value * value, axis=1, keepdims=True)
            left.append((value * gain_ref[:, pl.ds(start, HEAD_DIM)]).astype(BF16))
            right.append(
                jnp.concatenate(
                    [w_buf[i, pl.ds(start, HEAD_DIM), :] for i in range(4)], axis=1
                )
            )
        square_buf[g] = square.reshape(g.size, most * group_rows, 1)
        acc_buf[g] += jnp.dot(
            jnp.concatenate(left, axis=1),
            jnp.concatenate(right, axis=0),
            preferred_element_type=F32,
        ).reshape(g.size, most * group_rows, 4 * units)

    order = (0, 3, 1, 2)
    near_parts = [(y, t)] + list(arrivals[:5])
    far_parts = list(arrivals[5:])
    last = order[-1]

    planes(0)
    with mark("collect0"):
        collect(0)
    first_stage(0)
    planes(1)
    planes(2)
    with mark("collect3"):
        collect(3)
    first_stage(3)
    with mark("second0"):
        second_stage(0, groups_of(0)[0])
    with mark("collect1"):
        collect(1)
    first_stage(1)
    planes(3)
    with mark("second3"):
        second_stage(3, groups_of(3)[0])
    with mark("collect2"):
        collect(2)
    first_stage(2)
    with mark("second1"):
        second_stage(1, groups_of(1)[0])
    acc_buf[...] = jnp.zeros_like(acc_buf)
    square_buf[...] = jnp.zeros_like(square_buf)
    with mark("weights"):
        for i, (_, ref) in enumerate(
            ((gate_ref, w_buf.at[co]), (up_ref, w_buf.at[2 + co]), (down_ref, d_buf.at[co]))
        ):
            loaded(weights[i][1], weight_s.at[i])
            got(ref, weight_r.at[i])
    for h in order[:2]:
        g = groups_of(h)[0]
        with mark(f"feat{h}"):
            near(h, g)
            far(h, g)
        with mark(f"expert{h}"):
            expert_parts(near_parts + far_parts, h, g)
    g0, g1 = groups_of(last)
    with mark("secondL0"):
        second_stage(last, g0)
    g = groups_of(1)[0]
    with mark("feat1"):
        near(1, g)
        far(1, g)
    with mark("secondL1"):
        second_stage(last, g1)
    with mark("expert1"):
        expert_parts(near_parts + far_parts, 1, g)
    for g in (g0, g1):
        with mark(f"nearL{g.start}"):
            near(last, g)
        with mark(f"farL{g.start}"):
            far(last, g)
        with mark(f"expertL{g.start}"):
            expert_parts(near_parts + far_parts, last, g)
            i = g.start
            scale = lax.rsqrt(square_buf[i] * (1.0 / features) + epsilon)
            gate_val = acc_buf[i, :, pl.ds(0, 2 * units)] * scale
            up_val = acc_buf[i, :, pl.ds(2 * units, 2 * units)] * scale
            hid_buf[x, i] = (gate_val / (1.0 + jnp.exp(-gate_val)) * up_val).astype(BF16)
        push(hid_buf.at[x, i], hid_buf.at[x, i], hid_r.at[i], dev_x)

    wide = half // SPAN
    pieces = [(s, j) for s in range(2) for j in range(wide)]
    per = SPAN // HEAD_DIM

    def chunk(i, s, j):
        return (i * 2 + s) * wide + j

    def branch(i, s, which, j):
        hidden = jnp.concatenate([hid_buf[n, i] for n in range(2)], axis=1)
        at = pl.ds(pl.multiple_of(which * half + j * SPAN, SPAN), SPAN)
        weight = d_buf[c if s == 0 else co, :, at]
        return jnp.dot(hidden, weight, preferred_element_type=F32).astype(BF16)

    def down(i):
        with mark(f"hid{i}"):
            got(hid_buf.at[xo, i], hid_r.at[i])
        with mark(f"down{i}"):
            for s, j in pieces:
                k = chunk(i, s, j)
                b_out[k] = branch(i, s, yo, j)
                push(b_out.at[k], b_in.at[k], branch_r.at[k], dev_y)
            for s, j in pieces:
                k = chunk(i, s, j)
                stream = jnp.concatenate(
                    [x_buf[y, t if s == 0 else tc, j * per + m, i] for m in range(per)], axis=1
                )
                part[k] = stream.astype(F32) + branch(i, s, y, j).astype(F32)

    def blend(k):
        with mark(f"blend{k}"):
            got(b_in.at[k], branch_r.at[k])
            total = part[k] + b_in[k].astype(F32)
            mix[k][...] = total.astype(BF16).reshape(most, group_rows, SPAN)
        for plane, device in ((0, dev_up), (PLANES - 1, dev_dn)):

            @pl.when(z == plane)
            def _():
                push_plane(plane, mix[k], end_in[k], end_r.at[k], device)

    def pick(flag, a, b):
        mask = jnp.full(a.shape, flag.astype(jnp.int32), jnp.int32) > 0
        return jnp.where(mask, a.astype(F32), b.astype(F32)).astype(BF16)

    def give(here, way, k, d, other):
        out, arrived = (up_out, up_in) if way == 0 else (dn_out, dn_in)
        for n in range(2):
            b = 2 * d + n
            out[k, d, n] = pick(expert[b] == here, mix[k][slot[b]], other(b, n))
        push_plane(
            here,
            out.at[k, d],
            arrived.at[k, d],
            ret_r.at[d % 2, k],
            dev_up if way == 0 else dev_dn,
        )

    def turn_in(k):
        for here, way, targets in ((1, 0, (3, 2)), (2, 1, (0, 1))):

            @pl.when(z == here)
            def _():
                with mark(f"turn{k}"):
                    got(end_in[k], end_r.at[k])
                for d in targets:
                    give(here, way, k, d, lambda b, n: end_in[k][slot[b]])

    def carry(k):
        for here, way, d, arrived in ((2, 0, 3, up_in), (1, 1, 0, dn_in)):

            @pl.when(z == here)
            def _():
                with mark(f"carry{k}"):
                    got(arrived.at[k, d], ret_r.at[d % 2, k])
                give(here, way, k, d, lambda b, n: arrived[k, d, n])

    def target(side, i, which, j):
        return out_ref.at[
            pl.ds(pl.multiple_of(side * core_rows + i * group_rows, group_rows), group_rows),
            pl.ds(pl.multiple_of(which * half + j * SPAN, SPAN), SPAN),
        ]

    def arrive(i, s, j):
        k = chunk(i, s, j)
        for d in range(PLANES):

            @pl.when(z == d)
            def _():
                with mark(f"arrive{k}"):
                    if d > 1:
                        got(up_in.at[k, d], ret_r.at[d % 2, k])
                    if d < PLANES - 2:
                        got(dn_in.at[k, d], ret_r.at[d % 2, k])
                for n in range(2):
                    b = 2 * d + n
                    value = mix[k][slot[b]]
                    if d > 0:
                        lower = up_in[k, d, n] if d > 1 else end_in[k][slot[b]]
                        value = pick(expert[b] < d, lower, value)
                    if d < PLANES - 1:
                        higher = dn_in[k, d, n] if d < PLANES - 2 else end_in[k][slot[b]]
                        value = pick(expert[b] > d, higher, value)
                    fin[k, n] = value

        mine = target(c, i, y, j)
        push(fin.at[k, yo], mine, last_r.at[0], dev_y if s == 0 else dev_yc)
        if s == 0:
            mine[...] = fin[k, y]
        else:
            push(fin.at[k, y], mine, last_r.at[0], dev_c)

    down(0)
    first_chunks = [chunk(0, s, j) for s, j in pieces]
    second_chunks = [chunk(1, s, j) for s, j in pieces]
    for k in first_chunks:
        blend(k)
    down(1)
    for k in first_chunks[:2]:
        turn_in(k)
    for k in second_chunks:
        blend(k)
    every = [(i, s, j) for i in range(GROUPS) for s, j in pieces]
    for k in first_chunks[2:]:
        turn_in(k)
    for n, (i, s, j) in enumerate(every):
        k = chunk(i, s, j)
        if n + 4 < len(every):
            turn_in(chunk(*every[n + 4]))
        carry(k)
        if n > 0:
            arrive(*every[n - 1])
    arrive(*every[-1])
    with mark("lastwait"):
        wait_for(3 * size_of(out_ref) // 4, last_r.at[0])

    def all_sent(sem, amount):
        if amount:
            ref = w_buf.at[0, pl.ds(0, amount // (2 * units))]
            remote(ref, ref, sem, hid_r.at[0], dev_y).wait_send()

    with mark("drain"):
        for lot, amount in enumerate(all_lots):
            all_sent(sent.at[lot], amount)
        for plane in range(PLANES):

            @pl.when(z == plane)
            def _():
                for lot, amount in enumerate(plane_lots[plane]):
                    all_sent(plane_sent.at[lot], amount)


def local(
    queries, keys, values, residual_in, norm_gain, routing, gate_weight, up_weight, down_weight
):
    seq_count = lax.axis_size("seq")
    tp_count = lax.axis_size("tp")
    rows, width = queries.shape
    units = gate_weight.shape[2]
    planes = seq_count // 2
    fits = (
        tp_count == 4
        and seq_count == 2 * PLANES
        and rows == BLOCK
        and WINDOW == 4 * rows
        and units == 128
        and width == 8 * HEAD_DIM
    )
    if not fits:
        return local_general(
            queries,
            keys,
            values,
            residual_in,
            norm_gain,
            routing,
            gate_weight,
            up_weight,
            down_weight,
        )
    half = width // 2
    heads = half // HEAD_DIM
    most = min(2 * seq_count // planes, seq_count - planes + 1)
    core_rows = rows // 2
    group_rows = core_rows // GROUPS
    wide = half // SPAN
    chunks = GROUPS * 2 * wide
    vmem = pl.BlockSpec(memory_space=pltpu.VMEM)
    anywhere = pl.BlockSpec(memory_space=pltpu.MemorySpace.HBM)
    dma = pltpu.SemaphoreType.DMA

    def room(*shape, kind=BF16):
        return pltpu.VMEM(shape, kind)

    scratch = (
        room(4, heads, 2, 2, rows, HEAD_DIM),
        room(2, heads, 2, 2, rows, HEAD_DIM),
        room(2, heads, 2, rows, HEAD_DIM),
        [room(2 * planes, 2, core_rows, HEAD_DIM) for _ in range(heads)],
        room(2, tp_count, heads, GROUPS, most * group_rows, HEAD_DIM),
        room(heads, GROUPS, most * group_rows, HEAD_DIM),
        room(4, gate_weight.shape[1], units),
        room(2, down_weight.shape[1], width),
        room(GROUPS, most * group_rows, 4 * units, kind=F32),
        room(GROUPS, most * group_rows, 1, kind=F32),
        room(2, GROUPS, most * group_rows, 2 * units),
        room(chunks, most * group_rows, SPAN),
        room(chunks, most * group_rows, SPAN),
        room(chunks, most * group_rows, SPAN, kind=F32),
        [room(most, group_rows, SPAN) for _ in range(chunks)],
        [room(most, group_rows, SPAN) for _ in range(chunks)],
        room(chunks, planes, 2, group_rows, SPAN),
        room(chunks, planes, 2, group_rows, SPAN),
        room(chunks, planes, 2, group_rows, SPAN),
        room(chunks, planes, 2, group_rows, SPAN),
        room(chunks, 2, group_rows, SPAN),
        dma((2, heads)),
        dma((2, heads)),
        dma((3,)),
        dma((2, heads)),
        dma((4, heads)),
        dma((heads,)),
        dma((planes, heads)),
        dma((4, heads + GROUPS - 1)),
        dma((3,)),
        dma((GROUPS,)),
        dma((chunks,)),
        dma((chunks,)),
        dma((2, chunks)),
        dma((1,)),
        dma((8,)),
        dma((4,)),
    )
    flat, tree = jax.tree.flatten(scratch, is_leaf=lambda leaf: not isinstance(leaf, (list, tuple)))

    def kernel(*refs):
        layer_kernel(most, refs[:9], refs[9], jax.tree.unflatten(tree, refs[10:]))

    return pl.pallas_call(
        kernel,
        name="layer",
        out_shape=jax.ShapeDtypeStruct((rows, width), BF16),
        in_specs=[pl.BlockSpec(memory_space=pltpu.SMEM)]
        + [anywhere] * 4
        + [vmem]
        + [anywhere] * 3,
        out_specs=vmem,
        scratch_shapes=flat,
        compiler_params=pltpu.CompilerParams(
            collective_id=0, has_side_effects=True, vmem_limit_bytes=67043328
        ),
    )(
        routing.reshape(-1),
        queries,
        keys,
        values,
        residual_in,
        norm_gain.reshape(1, -1),
        gate_weight,
        up_weight,
        down_weight,
    )


def solution(mesh):
    in_specs = (
        P("seq", "tp"),
        P("seq", "tp"),
        P("seq", "tp"),
        P("seq", "tp"),
        P(),
        P(),
        P("seq", None, "tp"),
        P("seq", None, "tp"),
        P("seq", None, "tp"),
    )
    out_specs = P("seq", "tp")
    return jax.shard_map(local, mesh=mesh, in_specs=in_specs, out_specs=out_specs, check_vma=False)
```

time: 103 us -> 84.9 us (0.82); the launches traced: 101 us -> 84.6 us
  Pallas kernels: 99.5 us -> 82.9 us
    pallas_call x1, Pallas kernels: 99.5 us -> 82.9 us  [local(): pl.pallas_call(kernel, name='layer', out_shape=jax.ShapeDtypeStruct((rows...]
where the time goes in v1:
time: 84.9 us; the launch traced here: 84.6 us
  Pallas kernels  82.9 us (98%)
  local copies, waits for them, and re-layouts  1.67 us (2%)
    pallas_call x1, Pallas kernels, local(): pl.pallas_call(kernel, name='layer', out_shape=jax.ShapeDtypeStruct((rows...  82.9 us

profile of v1, /device:TPU:1, one launch (start us, length us, event | category | flops | bytes accessed | tf_op | source)
XLA Modules:
  0.0 84.6 jit_solution(17658483416226568586)
XLA Ops:
  0.0 82.9 %layer.1 = bf16[128,1024]{1,0:T(8,128)(2,1)} custom-call(s32[8]{0:T(128)} %bitcast.3, bf16[128,1024]{1,0:T(8,128)(2,1)} %refs_1_.1, bf16[128,1024]{1,0:T(8,128)(2,1)} %refs_2_.1, bf16[128,1024]{1,0:T(8,128)(2,1)} %refs_3_.1, bf16[128,1024]{1,0:T(8,128)(2,1)} %refs_4_.1, f32[1,4096]{1,0:T(1,128)} %bitcast.2, bf16[1,4096,128]{2,1,0:T(8,128)(2,1)} %refs_6_.1, ...), custom_call_target="tpu_custom_call" | custom-call | tf_op jit(solution)/shard_map/layer/pallas_call | solution.py:932
  82.9 1.7 %copy.11 = bf16[128,1024]{1,0:T(8,128)(2,1)} copy(bf16[128,1024]{1,0:T(8,128)(2,1)} %layer.1) | data formatting | bytes 524288

commit v2 on v1

--- a/solution.py
+++ b/solution.py
@@ -124,7 +124,7 @@
 F32 = jnp.float32
 PLANES = 4
 GROUPS = 2
-SPAN = 2 * HEAD_DIM
+SPAN = HEAD_DIM
 STAY_HEAD = 3
 
 
@@ -176,7 +176,6 @@
         weight_s,
         swap_r,
         kv_r,
-        qr_r,
         line_r,
         feat_r,
         weight_r,
@@ -263,23 +262,21 @@
     def load_own(kind, h):
         for n, ref in enumerate(sources[kind]):
             pltpu.make_async_copy(
-                ref.at[:, cols(y, h)], place(kind, h, n, y), own_s.at[kind, h]
+                ref.at[:, cols(y, h)], place(kind, h, n, y), own_s.at[0]
             ).start()
 
     def load_away(kind, h):
         for n, ref in enumerate(sources[kind]):
             pltpu.make_async_copy(
-                ref.at[:, cols(yo, h)], away.at[kind, h, n], away_s.at[kind, h]
+                ref.at[:, cols(yo, h)], away.at[kind, h, n], away_s.at[0]
             ).start()
 
     def swap(kind, h):
-        loaded(away.at[kind, h], away_s.at[kind, h])
         buf = kv_buf if kind == 0 else qr_buf
         push(away.at[kind, h], buf.at[0, h, :, y], swap_r.at[kind, h], dev_y)
 
     def own(kind, h):
         buf = kv_buf if kind == 0 else qr_buf
-        loaded(buf.at[0, h, :, y], own_s.at[kind, h])
         got(buf.at[0, h, :, yo], swap_r.at[kind, h])
 
     for kind in range(2):
@@ -306,8 +303,11 @@
     with mark("barwait"):
         pl.semaphore_wait(barrier, 5 + jnp.where(has_up, 1, 0) + jnp.where(has_dn, 1, 0))
 
-    low_order = ((0, 3), (0, 0), (1, 3), (1, 0), (0, 1), (0, 2), (1, 1), (1, 2))
-    high_order = ((0, 0), (1, 0), (0, 1), (1, 1), (0, 3), (0, 2), (1, 2), (1, 3))
+    low_order = ((0, 3), (0, 0), (1, 3), (1, 0), (0, 1), (1, 1), (0, 2), (1, 2))
+    high_order = ((0, 0), (1, 0), (0, 3), (0, 1), (1, 1), (1, 3), (0, 2), (1, 2))
+
+    with mark("away"):
+        loaded(away, away_s.at[0])
 
     @pl.when(z < 2)
     def _():
@@ -326,10 +326,12 @@
         (up_ref.at[0], w_buf.at[2 + c]),
         (down_ref.at[0], d_buf.at[c]),
     )
-    for i, (src, dst) in enumerate(weights):
-        pltpu.make_async_copy(src, dst, weight_s.at[i]).start()
-        push(src, dst, weight_r.at[i], dev_c)
-
+    for src, dst in weights:
+        pltpu.make_async_copy(src, dst, weight_s.at[0]).start()
+        push(src, dst, weight_r.at[0], dev_c)
+
+    with mark("ownwait"):
+        loaded(away, own_s.at[0])
     row_at = lax.broadcasted_iota(jnp.int32, (rows, rows), 0)
     col_at = lax.broadcasted_iota(jnp.int32, (rows, rows), 1)
     below, above, farther = 1, 2, 3
@@ -379,17 +381,20 @@
     def device_at(way):
         return dev_up if way > 0 else dev_dn
 
+    def kv_sem(at, h):
+        return kv_r.at[2 * heads if at == farther else (at - 1) * heads + h]
+
     def send_kv(here, way, src, dst, h):
-        push_plane(here, kv_buf.at[src, h], kv_buf.at[dst, h], kv_r.at[dst, h], device_at(way))
+        push_plane(here, kv_buf.at[src, h], kv_buf.at[dst, h], kv_sem(dst, h), device_at(way))
 
     def got_kv(at, h):
-        got(kv_buf.at[at, h], kv_r.at[at, h])
+        got(kv_buf.at[at, h], kv_sem(at, h))
 
     def send_qr(here, h):
-        push_plane(here, qr_buf.at[0, h], qr_buf.at[1, h], qr_r.at[h], dev_dn)
-
-    def got_qr(h):
-        got(qr_buf.at[1, h], qr_r.at[h])
+        push_plane(here, qr_buf.at[0, h], qr_buf.at[1, h], kv_sem(above, h), dev_dn)
+
+    def got_above(h):
+        wait_for(size_of(kv_buf.at[0, h]) + size_of(qr_buf.at[0, h]), kv_sem(above, h))
 
     def send_line(here, way, plane, h):
         ref = line[h].at[pl.ds(2 * plane, 2)]
@@ -441,8 +446,7 @@
 
         def lower(h):
             with mark(f"lower{h}"):
-                got_kv(above, h)
-                got_qr(h)
+                got_above(h)
             made(1, 2, h)
 
         if step == 0:
@@ -452,22 +456,22 @@
             first(1)
             home(0)
             pass_on(1, 1, 0, 3)
-            first(2)
             lower(0)
             pass_on(1, 1, 0, 0)
+            first(2)
             home(1)
+            pass_on(1, -1, 3, 0)
             lower(1)
+        if step == 1:
             pass_on(1, 1, 0, 1)
+            pass_on(1, -1, 2, 3)
             home(2)
+            pass_on(1, -1, 3, 1)
+        if step == 2:
             pass_on(1, 1, 0, 2)
+            pass_on(1, -1, 3, 3)
+        if step == 3:
             lower(2)
-            pass_on(1, -1, 3, 0)
-        if step == 1:
-            pass_on(1, -1, 2, 3)
-            pass_on(1, -1, 3, 3)
-        if step == 2:
-            pass_on(1, -1, 3, 1)
-        if step == 3:
             pass_on(1, -1, 3, 2)
 
     def steps_2(step):
@@ -487,35 +491,40 @@
 
         def lower(h):
             with mark(f"lower{h}"):
-                got_kv(above, h)
+                got_above(h)
                 got_kv(below, h)
-                got_qr(h)
             made(2, 3, h)
 
         if step == 0:
-            for kind, h in high_order:
-                if (kind, h) == (1, 2):
-                    with mark("below3"):
-                        got_kv(below, 3)
-                    send_kv(2, 1, below, farther, 3)
-                (second if kind else first)(h)
+            first(0)
+            second(0)
+            first(3)
+            first(1)
+            with mark("below3"):
+                got_kv(below, 3)
+            send_kv(2, 1, below, farther, 3)
+            second(1)
+            second(3)
             lower(0)
             with mark("farther3"):
                 got_kv(farther, 3)
             made(2, 2, 3)
             pass_on(2, 1, 1, 3)
             lower(1)
+            pass_on(2, -1, 3, 3)
+            first(2)
+            second(2)
+            pass_on(2, 1, 1, 0)
             pass_on(2, 1, 0, 3)
-            pass_on(2, 1, 1, 0)
-            lower(2)
+        if step == 1:
+            pass_on(2, 1, 2, 0)
             pass_on(2, 1, 0, 0)
-            pass_on(2, -1, 3, 3)
-            pass_on(2, 1, 2, 0)
         if step == 2:
             pass_on(2, 1, 1, 1)
+            pass_on(2, 1, 2, 1)
             pass_on(2, 1, 0, 1)
-            pass_on(2, 1, 2, 1)
         if step == 3:
+            lower(2)
             pass_on(2, 1, 1, 2)
             pass_on(2, 1, 0, 2)
             pass_on(2, 1, 2, 2)
@@ -530,10 +539,11 @@
                         send_kv(3, -1, 0, above, h)
                     else:
                         send_qr(3, h)
-            with mark("below3"):
-                got_kv(below, 3)
-                got_kv(farther, 3)
-            made(3, 3, 3)
+                elif kind == 1:
+                    with mark("below3"):
+                        got_kv(below, 3)
+                        got_kv(farther, 3)
+                    made(3, 3, 3)
 
     def planes(step):
         for plane, steps in enumerate((steps_0, steps_1, steps_2, steps_3)):
@@ -542,8 +552,11 @@
             def _():
                 steps(step)
 
-    def collect(h):
+    def collect(order, pos):
+        h = order[pos]
         for plane in range(PLANES):
+            if orders[plane // 2][pos] != h:
+                continue
 
             @pl.when(z == plane)
             def _():
@@ -552,15 +565,20 @@
                         taken[plane].add((other, h))
                         got_line(other, h)
 
-    def groups_of(h):
-        return [pl.ds(g, 1) for g in range(GROUPS)] if h == order[-1] else [pl.ds(0, GROUPS)]
-
-    def feature_at(h, g):
-        return order.index(h) + g.start
-
-    def feature(n, py, pt, h, g, device, src=None):
-        ref = x_buf.at[py, pt, h, g]
-        push(ref if src is None else src, ref, feat_r.at[lot_of[n], feature_at(h, g)], device)
+    high = jnp.where(z < 2, 0, 1)
+    orders = ((0, 1, 3, 2), (3, 0, 1, 2))
+    heads_at = [low + high * (up - low) for low, up in zip(*orders)]
+    ends = len(heads_at) - 1
+
+    def groups_of(pos):
+        return [pl.ds(g, 1) for g in range(GROUPS)] if pos == ends else [pl.ds(0, GROUPS)]
+
+    def feature_at(pos, g):
+        return pos + g.start
+
+    def feature(n, py, pt, pos, g, device, src=None):
+        ref = x_buf.at[py, pt, heads_at[pos], g]
+        push(ref if src is None else src, ref, feat_r.at[lot_of[n], feature_at(pos, g)], device)
 
     lot_of = (0, 0, 1, 2, 0, 3, 3)
     arrivals = (
@@ -573,45 +591,58 @@
         (yo, txc),
     )
 
-    def take(n, h, g):
+    def take(n, pos, g):
         py, pt = arrivals[n]
-        got(x_buf.at[py, pt, h, g], feat_r.at[lot_of[n], feature_at(h, g)])
-
-    def first_stage(h):
-        for g in groups_of(h):
-            for r in range(most):
-                at = pl.ds(r * group_rows, group_rows)
-                for ref, side in ((x_buf.at[y, t, h], c), (x_other.at[h], co)):
-                    block = line[h][chosen[r], side]
-                    for i in range(GROUPS):
-                        if g.start <= i < g.start + g.size:
-                            ref[i, at] = block[i * group_rows : (i + 1) * group_rows]
-            other = x_other.at[h, g]
-            feature(3, y, t, h, g, dev_y)
-            feature(2, y, t, h, g, dev_xc, other)
-            feature(1, y, t, h, g, dev_x)
-            feature(4, y, t, h, g, dev_yc, other)
-            feature(0, y, t, h, g, dev_c, other)
-
-    def second_stage(h, g):
-        take(3, h, g)
-        feature(5, yo, t, h, g, dev_x)
-        take(2, h, g)
-        feature(6, y, txc, h, g, dev_y)
-
-    def near(h, g):
-        wait_for(3 * size_of(x_buf.at[y, t, h, g]), feat_r.at[0, feature_at(h, g)])
-
-    def far(h, g):
-        wait_for(2 * size_of(x_buf.at[y, t, h, g]), feat_r.at[3, feature_at(h, g)])
-
-    def expert_parts(parts, h, g):
+        got(x_buf.at[py, pt, heads_at[pos], g], feat_r.at[lot_of[n], feature_at(pos, g)])
+
+    def choose(h, g):
+        for r in range(most):
+            at = pl.ds(r * group_rows, group_rows)
+            for ref, side in ((x_buf.at[y, t, h], c), (x_other.at[h], co)):
+                block = line[h][chosen[r], side]
+                for i in range(GROUPS):
+                    if g.start <= i < g.start + g.size:
+                        ref[i, at] = block[i * group_rows : (i + 1) * group_rows]
+
+    def gather(pos):
+        with mark(f"collect{pos}"):
+            for order in orders:
+                if order is orders[0] or order[pos] != orders[0][pos]:
+                    collect(order, pos)
+
+    def first_stage(pos, lots=None):
+        for g in lots or groups_of(pos):
+            if orders[0][pos] == orders[1][pos]:
+                choose(orders[0][pos], g)
+            else:
+                pl.when(z < 2)(lambda: choose(orders[0][pos], g))
+                pl.when(z >= 2)(lambda: choose(orders[1][pos], g))
+            other = x_other.at[heads_at[pos], g]
+            feature(3, y, t, pos, g, dev_y)
+            feature(2, y, t, pos, g, dev_xc, other)
+            feature(1, y, t, pos, g, dev_x)
+            feature(4, y, t, pos, g, dev_yc, other)
+            feature(0, y, t, pos, g, dev_c, other)
+
+    def second_stage(pos, g):
+        take(3, pos, g)
+        feature(5, yo, t, pos, g, dev_x)
+        take(2, pos, g)
+        feature(6, y, txc, pos, g, dev_y)
+
+    def near(pos, g):
+        wait_for(3 * size_of(x_buf.at[y, t, 0, g]), feat_r.at[0, feature_at(pos, g)])
+
+    def far(pos, g):
+        wait_for(2 * size_of(x_buf.at[y, t, 0, g]), feat_r.at[3, feature_at(pos, g)])
+
+    def expert_parts(parts, pos, g):
         depth = g.size * most * group_rows
         left, right = [], []
         square = square_buf[g].reshape(depth, 1)
         for py, pt in parts:
-            start = pl.multiple_of((2 * pt + py) * half + h * HEAD_DIM, HEAD_DIM)
-            value = x_buf[py, pt, h, g].reshape(depth, HEAD_DIM).astype(F32)
+            start = pl.multiple_of((2 * pt + py) * half + heads_at[pos] * HEAD_DIM, HEAD_DIM)
+            value = x_buf[py, pt, heads_at[pos], g].reshape(depth, HEAD_DIM).astype(F32)
             square = square + jnp.sum(value * value, axis=1, keepdims=True)
             left.append((value * gain_ref[:, pl.ds(start, HEAD_DIM)]).astype(BF16))
             right.append(
@@ -626,66 +657,57 @@
             preferred_element_type=F32,
         ).reshape(g.size, most * group_rows, 4 * units)
 
-    order = (0, 3, 1, 2)
-    near_parts = [(y, t)] + list(arrivals[:5])
-    far_parts = list(arrivals[5:])
-    last = order[-1]
-
+    every_part = [(y, t)] + list(arrivals)
+
+    g0, g1 = groups_of(ends)
+    both = groups_of(0)[0]
     planes(0)
-    with mark("collect0"):
-        collect(0)
+    gather(0)
     first_stage(0)
     planes(1)
+    gather(1)
+    first_stage(1)
+    with mark("second0"):
+        second_stage(0, both)
     planes(2)
-    with mark("collect3"):
-        collect(3)
-    first_stage(3)
-    with mark("second0"):
-        second_stage(0, groups_of(0)[0])
-    with mark("collect1"):
-        collect(1)
-    first_stage(1)
-    planes(3)
-    with mark("second3"):
-        second_stage(3, groups_of(3)[0])
-    with mark("collect2"):
-        collect(2)
+    gather(2)
     first_stage(2)
     with mark("second1"):
-        second_stage(1, groups_of(1)[0])
+        second_stage(1, both)
+    planes(3)
+    gather(3)
+    first_stage(3, [g0])
+    with mark("second2"):
+        second_stage(2, both)
+    first_stage(3, [g1])
     acc_buf[...] = jnp.zeros_like(acc_buf)
     square_buf[...] = jnp.zeros_like(square_buf)
     with mark("weights"):
-        for i, (_, ref) in enumerate(
-            ((gate_ref, w_buf.at[co]), (up_ref, w_buf.at[2 + co]), (down_ref, d_buf.at[co]))
-        ):
-            loaded(weights[i][1], weight_s.at[i])
-            got(ref, weight_r.at[i])
-    for h in order[:2]:
-        g = groups_of(h)[0]
-        with mark(f"feat{h}"):
-            near(h, g)
-            far(h, g)
-        with mark(f"expert{h}"):
-            expert_parts(near_parts + far_parts, h, g)
-    g0, g1 = groups_of(last)
+        every = w_buf.at[pl.ds(0, len(weights))]
+        loaded(every, weight_s.at[0])
+        got(every, weight_r.at[0])
+
+    def whole(pos):
+        with mark(f"feat{pos}"):
+            near(pos, both)
+            far(pos, both)
+        with mark(f"expert{pos}"):
+            expert_parts(every_part, pos, both)
+
+    whole(0)
     with mark("secondL0"):
-        second_stage(last, g0)
-    g = groups_of(1)[0]
-    with mark("feat1"):
-        near(1, g)
-        far(1, g)
+        second_stage(ends, g0)
     with mark("secondL1"):
-        second_stage(last, g1)
-    with mark("expert1"):
-        expert_parts(near_parts + far_parts, 1, g)
+        second_stage(ends, g1)
+    whole(1)
+    whole(2)
     for g in (g0, g1):
         with mark(f"nearL{g.start}"):
-            near(last, g)
+            near(ends, g)
         with mark(f"farL{g.start}"):
-            far(last, g)
+            far(ends, g)
         with mark(f"expertL{g.start}"):
-            expert_parts(near_parts + far_parts, last, g)
+            expert_parts(every_part, ends, g)
             i = g.start
             scale = lax.rsqrt(square_buf[i] * (1.0 / features) + epsilon)
             gate_val = acc_buf[i, :, pl.ds(0, 2 * units)] * scale
@@ -695,33 +717,35 @@
 
     wide = half // SPAN
     pieces = [(s, j) for s in range(2) for j in range(wide)]
-    per = SPAN // HEAD_DIM
 
     def chunk(i, s, j):
         return (i * 2 + s) * wide + j
 
+    pair = 2 * SPAN
+
     def branch(i, s, which, j):
         hidden = jnp.concatenate([hid_buf[n, i] for n in range(2)], axis=1)
-        at = pl.ds(pl.multiple_of(which * half + j * SPAN, SPAN), SPAN)
+        at = pl.ds(pl.multiple_of(which * half + j * pair, pair), pair)
         weight = d_buf[c if s == 0 else co, :, at]
-        return jnp.dot(hidden, weight, preferred_element_type=F32).astype(BF16)
+        value = jnp.dot(hidden, weight, preferred_element_type=F32).astype(BF16)
+        return [(chunk(i, s, 2 * j + m), value[:, m * SPAN : (m + 1) * SPAN]) for m in range(2)]
 
     def down(i):
         with mark(f"hid{i}"):
             got(hid_buf.at[xo, i], hid_r.at[i])
         with mark(f"down{i}"):
-            for s, j in pieces:
-                k = chunk(i, s, j)
-                b_out[k] = branch(i, s, yo, j)
-                push(b_out.at[k], b_in.at[k], branch_r.at[k], dev_y)
-            for s, j in pieces:
-                k = chunk(i, s, j)
-                stream = jnp.concatenate(
-                    [x_buf[y, t if s == 0 else tc, j * per + m, i] for m in range(per)], axis=1
-                )
-                part[k] = stream.astype(F32) + branch(i, s, y, j).astype(F32)
-
-    def blend(k):
+            doubles = [(s, j) for s in range(2) for j in range(wide // 2)]
+            for s, j in doubles:
+                for k, value in branch(i, s, yo, j):
+                    b_out[k] = value
+                    push(b_out.at[k], b_in.at[k], branch_r.at[k], dev_y)
+            for s, j in doubles:
+                for m, (k, value) in enumerate(branch(i, s, y, j)):
+                    stream = x_buf[y, t if s == 0 else tc, 2 * j + m, i]
+                    part[k] = stream.astype(F32) + value.astype(F32)
+
+    def blend(i, s, j):
+        k = chunk(i, s, j)
         with mark(f"blend{k}"):
             got(b_in.at[k], branch_r.at[k])
             total = part[k] + b_in[k].astype(F32)
@@ -749,7 +773,8 @@
             dev_up if way == 0 else dev_dn,
         )
 
-    def turn_in(k):
+    def turn_in(i, s, j):
+        k = chunk(i, s, j)
         for here, way, targets in ((1, 0, (3, 2)), (2, 1, (0, 1))):
 
             @pl.when(z == here)
@@ -759,7 +784,8 @@
                 for d in targets:
                     give(here, way, k, d, lambda b, n: end_in[k][slot[b]])
 
-    def carry(k):
+    def carry(i, s, j):
+        k = chunk(i, s, j)
         for here, way, d, arrived in ((2, 0, 3, up_in), (1, 1, 0, dn_in)):
 
             @pl.when(z == here)
@@ -803,27 +829,14 @@
         else:
             push(fin.at[k, y], mine, last_r.at[0], dev_c)
 
-    down(0)
-    first_chunks = [chunk(0, s, j) for s, j in pieces]
-    second_chunks = [chunk(1, s, j) for s, j in pieces]
-    for k in first_chunks:
-        blend(k)
-    down(1)
-    for k in first_chunks[:2]:
-        turn_in(k)
-    for k in second_chunks:
-        blend(k)
     every = [(i, s, j) for i in range(GROUPS) for s, j in pieces]
-    for k in first_chunks[2:]:
-        turn_in(k)
-    for n, (i, s, j) in enumerate(every):
-        k = chunk(i, s, j)
-        if n + 4 < len(every):
-            turn_in(chunk(*every[n + 4]))
-        carry(k)
-        if n > 0:
-            arrive(*every[n - 1])
-    arrive(*every[-1])
+    for i in range(GROUPS):
+        down(i)
+    stages = ((0, blend), (4, turn_in), (8, carry), (11, arrive))
+    for n in range(len(every) + stages[-1][0]):
+        for lag, stage in stages:
+            if 0 <= n - lag < len(every):
+                stage(*every[n - lag])
     with mark("lastwait"):
         wait_for(3 * size_of(out_ref) // 4, last_r.at[0])
 
@@ -907,15 +920,14 @@
         room(chunks, planes, 2, group_rows, SPAN),
         room(chunks, planes, 2, group_rows, SPAN),
         room(chunks, 2, group_rows, SPAN),
+        dma((1,)),
+        dma((1,)),
+        dma((1,)),
         dma((2, heads)),
-        dma((2, heads)),
-        dma((3,)),
-        dma((2, heads)),
-        dma((4, heads)),
-        dma((heads,)),
+        dma((2 * heads + 1,)),
         dma((planes, heads)),
         dma((4, heads + GROUPS - 1)),
-        dma((3,)),
+        dma((1,)),
         dma((GROUPS,)),
         dma((chunks,)),
         dma((chunks,)),

time: 84.9 us -> 83.3 us (0.981)
  Pallas kernels: 82.9 us -> 81.4 us
    pallas_call x1, Pallas kernels: 82.9 us -> 81.4 us  [local(): pl.pallas_call(kernel, name='layer', out_shape=jax.ShapeDtypeStruct((rows...]
where the time goes in v2:
time: 83.3 us; the launch traced here: 83.1 us
  Pallas kernels  81.4 us (98%)
  local copies, waits for them, and re-layouts  1.67 us (2%)
    pallas_call x1, Pallas kernels, local(): pl.pallas_call(kernel, name='layer', out_shape=jax.ShapeDtypeStruct((rows...  81.4 us
    unnamed x1, local copies, waits for them, and re-layouts  1.67 us

profile of v2, /device:TPU:1, one launch (start us, length us, event | category | flops | bytes accessed | tf_op | source)
XLA Modules:
  0.0 83.1 jit_solution(16575488519738472947)
XLA Ops:
  0.0 81.4 %layer.1 = bf16[128,1024]{1,0:T(8,128)(2,1)} custom-call(s32[8]{0:T(128)} %bitcast.3, bf16[128,1024]{1,0:T(8,128)(2,1)} %refs_1_.1, bf16[128,1024]{1,0:T(8,128)(2,1)} %refs_2_.1, bf16[128,1024]{1,0:T(8,128)(2,1)} %refs_3_.1, bf16[128,1024]{1,0:T(8,128)(2,1)} %refs_4_.1, f32[1,4096]{1,0:T(1,128)} %bitcast.2, bf16[1,4096,128]{2,1,0:T(8,128)(2,1)} %refs_6_.1, ...), custom_call_target="tpu_custom_call" | custom-call | tf_op jit(solution)/shard_map/layer/pallas_call | solution.py:944
  81.4 1.7 %copy.11 = bf16[128,1024]{1,0:T(8,128)(2,1)} copy(bf16[128,1024]{1,0:T(8,128)(2,1)} %layer.1) | data formatting | bytes 524288

commit v3 on v2

--- a/solution.py
+++ b/solution.py
@@ -221,8 +221,10 @@
         lots[-1] += size_of(ref)
         return len(lots) - 1
 
-    def push(src, dst, recv_sem, device):
-        lot = lot_for(all_lots, src)
+    final_lot = sent.shape[0] - 1
+
+    def push(src, dst, recv_sem, device, lot=None):
+        lot = lot_for(all_lots, src) if lot is None else lot
         remote(src, dst, sent.at[lot], recv_sem, device).start()
 
     def push_plane(plane, src, dst, recv_sem, device):
@@ -320,15 +322,6 @@
     def _():
         for kind, h in high_order:
             swap(kind, h)
-
-    weights = (
-        (gate_ref.at[0], w_buf.at[c]),
-        (up_ref.at[0], w_buf.at[2 + c]),
-        (down_ref.at[0], d_buf.at[c]),
-    )
-    for src, dst in weights:
-        pltpu.make_async_copy(src, dst, weight_s.at[0]).start()
-        push(src, dst, weight_r.at[0], dev_c)
 
     with mark("ownwait"):
         loaded(away, own_s.at[0])
@@ -390,8 +383,16 @@
     def got_kv(at, h):
         got(kv_buf.at[at, h], kv_sem(at, h))
 
-    def send_qr(here, h):
-        push_plane(here, qr_buf.at[0, h], qr_buf.at[1, h], kv_sem(above, h), dev_dn)
+    def send_part(here, way, kind, h, block):
+        at = below if way > 0 else above
+        buf, to = (kv_buf, at) if kind == 0 else (qr_buf, 1)
+        push_plane(
+            here, buf.at[0, h, :, block], buf.at[to, h, :, block], kv_sem(at, h), device_at(way)
+        )
+
+    def send_home(here, way, h, kinds=(0,)):
+        for kind in kinds:
+            send_part(here, way, kind, h, y)
 
     def got_above(h):
         wait_for(size_of(kv_buf.at[0, h]) + size_of(qr_buf.at[0, h]), kv_sem(above, h))
@@ -426,7 +427,7 @@
                 with mark(f"own{kind}_{h}"):
                     own(kind, h)
                 if kind == 0:
-                    send_kv(0, 1, 0, below, h)
+                    send_part(0, 1, 0, h, yo)
                 else:
                     made(0, 0, h)
 
@@ -434,7 +435,7 @@
         def first(h):
             with mark(f"own0_{h}"):
                 own(0, h)
-            send_kv(1, 1, 0, below, h)
+            send_part(1, 1, 0, h, yo)
 
         def home(h):
             with mark(f"own1_{h}"):
@@ -453,41 +454,38 @@
             first(3)
             first(0)
             home(3)
+            home(0)
             first(1)
-            home(0)
+            lower(0)
             pass_on(1, 1, 0, 3)
-            lower(0)
             pass_on(1, 1, 0, 0)
             first(2)
             home(1)
+            lower(1)
             pass_on(1, -1, 3, 0)
-            lower(1)
         if step == 1:
             pass_on(1, 1, 0, 1)
+            home(2)
+            pass_on(1, 1, 0, 2)
+            lower(2)
+            pass_on(1, -1, 3, 1)
+        if step == 3:
             pass_on(1, -1, 2, 3)
-            home(2)
-            pass_on(1, -1, 3, 1)
-        if step == 2:
-            pass_on(1, 1, 0, 2)
             pass_on(1, -1, 3, 3)
-        if step == 3:
-            lower(2)
+        if step == 4:
             pass_on(1, -1, 3, 2)
 
     def steps_2(step):
         def first(h):
             with mark(f"own0_{h}"):
                 own(0, h)
-            if h == STAY_HEAD:
-                send_kv(2, 1, 0, below, h)
-            else:
-                send_kv(2, -1, 0, above, h)
+            send_part(2, 1 if h == STAY_HEAD else -1, 0, h, yo)
 
         def second(h):
             with mark(f"own1_{h}"):
                 own(1, h)
             if h != STAY_HEAD:
-                send_qr(2, h)
+                send_part(2, -1, 1, h, yo)
 
         def lower(h):
             with mark(f"lower{h}"):
@@ -498,33 +496,35 @@
         if step == 0:
             first(0)
             second(0)
+            send_home(2, -1, 2, (0, 1))
             first(3)
             first(1)
             with mark("below3"):
                 got_kv(below, 3)
             send_kv(2, 1, below, farther, 3)
             second(1)
+            lower(0)
             second(3)
-            lower(0)
+            first(2)
             with mark("farther3"):
                 got_kv(farther, 3)
+            second(2)
             made(2, 2, 3)
             pass_on(2, 1, 1, 3)
             lower(1)
             pass_on(2, -1, 3, 3)
-            first(2)
-            second(2)
             pass_on(2, 1, 1, 0)
             pass_on(2, 1, 0, 3)
         if step == 1:
             pass_on(2, 1, 2, 0)
             pass_on(2, 1, 0, 0)
         if step == 2:
+            lower(2)
             pass_on(2, 1, 1, 1)
             pass_on(2, 1, 2, 1)
+        if step == 3:
             pass_on(2, 1, 0, 1)
-        if step == 3:
-            lower(2)
+        if step == 4:
             pass_on(2, 1, 1, 2)
             pass_on(2, 1, 0, 2)
             pass_on(2, 1, 2, 2)
@@ -535,15 +535,27 @@
                 with mark(f"own{kind}_{h}"):
                     own(kind, h)
                 if h != STAY_HEAD:
-                    if kind == 0:
-                        send_kv(3, -1, 0, above, h)
-                    else:
-                        send_qr(3, h)
+                    send_part(3, -1, kind, h, yo)
+                    if (kind, h) == (1, 0):
+                        send_home(3, -1, 2, (0, 1))
                 elif kind == 1:
                     with mark("below3"):
                         got_kv(below, 3)
                         got_kv(farther, 3)
                     made(3, 3, 3)
+
+    def early(plane):
+        if plane < 2:
+            for h in (3, 0, 1, 2):
+                send_home(plane, 1, h)
+        else:
+            for h in (0, 1):
+                send_home(plane, -1, h, (0, 1))
+            if plane == 2:
+                send_home(plane, 1, STAY_HEAD)
+
+    for plane in range(PLANES):
+        pl.when(z == plane)(lambda: early(plane))
 
     def planes(step):
         for plane, steps in enumerate((steps_0, steps_1, steps_2, steps_3)):
@@ -662,19 +674,29 @@
     g0, g1 = groups_of(ends)
     both = groups_of(0)[0]
     planes(0)
+    weights = (
+        (gate_ref.at[0], w_buf.at[c]),
+        (up_ref.at[0], w_buf.at[2 + c]),
+        (down_ref.at[0], d_buf.at[c]),
+    )
+    for src, dst in weights:
+        pltpu.make_async_copy(src, dst, weight_s.at[0]).start()
+        push(src, dst, weight_r.at[0], dev_c)
+
     gather(0)
     first_stage(0)
     planes(1)
     gather(1)
     first_stage(1)
+    planes(2)
     with mark("second0"):
         second_stage(0, both)
-    planes(2)
+    planes(3)
     gather(2)
     first_stage(2)
     with mark("second1"):
         second_stage(1, both)
-    planes(3)
+    planes(4)
     gather(3)
     first_stage(3, [g0])
     with mark("second2"):
@@ -800,39 +822,46 @@
             pl.ds(pl.multiple_of(which * half + j * SPAN, SPAN), SPAN),
         ]
 
-    def arrive(i, s, j):
+    def arrive(i, s, j, d):
         k = chunk(i, s, j)
-        for d in range(PLANES):
-
-            @pl.when(z == d)
-            def _():
-                with mark(f"arrive{k}"):
-                    if d > 1:
-                        got(up_in.at[k, d], ret_r.at[d % 2, k])
-                    if d < PLANES - 2:
-                        got(dn_in.at[k, d], ret_r.at[d % 2, k])
-                for n in range(2):
-                    b = 2 * d + n
-                    value = mix[k][slot[b]]
-                    if d > 0:
-                        lower = up_in[k, d, n] if d > 1 else end_in[k][slot[b]]
-                        value = pick(expert[b] < d, lower, value)
-                    if d < PLANES - 1:
-                        higher = dn_in[k, d, n] if d < PLANES - 2 else end_in[k][slot[b]]
-                        value = pick(expert[b] > d, higher, value)
-                    fin[k, n] = value
-
-        mine = target(c, i, y, j)
-        push(fin.at[k, yo], mine, last_r.at[0], dev_y if s == 0 else dev_yc)
-        if s == 0:
-            mine[...] = fin[k, y]
-        else:
-            push(fin.at[k, y], mine, last_r.at[0], dev_c)
+
+        @pl.when(z == d)
+        def _():
+            with mark(f"arrive{k}"):
+                if d > 1:
+                    got(up_in.at[k, d], ret_r.at[d % 2, k])
+                if d < PLANES - 2:
+                    got(dn_in.at[k, d], ret_r.at[d % 2, k])
+            for n in range(2):
+                b = 2 * d + n
+                value = mix[k][slot[b]]
+                if d > 0:
+                    lower = up_in[k, d, n] if d > 1 else end_in[k][slot[b]]
+                    value = pick(expert[b] < d, lower, value)
+                if d < PLANES - 1:
+                    higher = dn_in[k, d, n] if d < PLANES - 2 else end_in[k][slot[b]]
+                    value = pick(expert[b] > d, higher, value)
+                fin[k, n] = value
+            mine = target(c, i, y, j)
+            device = dev_y if s == 0 else dev_yc
+            push(fin.at[k, yo], mine, last_r.at[0], device, final_lot)
+            if s == 0:
+                mine[...] = fin[k, y]
+            else:
+                push(fin.at[k, y], mine, last_r.at[0], dev_c, final_lot)
+
+    def arrive_end(i, s, j):
+        arrive(i, s, j, 0)
+        arrive(i, s, j, PLANES - 1)
+
+    def arrive_middle(i, s, j):
+        arrive(i, s, j, 1)
+        arrive(i, s, j, 2)
 
     every = [(i, s, j) for i in range(GROUPS) for s, j in pieces]
     for i in range(GROUPS):
         down(i)
-    stages = ((0, blend), (4, turn_in), (8, carry), (11, arrive))
+    stages = ((0, blend), (4, turn_in), (9, carry), (12, arrive_middle), (16, arrive_end))
     for n in range(len(every) + stages[-1][0]):
         for lag, stage in stages:
             if 0 <= n - lag < len(every):
@@ -848,6 +877,7 @@
     with mark("drain"):
         for lot, amount in enumerate(all_lots):
             all_sent(sent.at[lot], amount)
+        all_sent(sent.at[final_lot], 3 * size_of(out_ref) // 4)
         for plane in range(PLANES):
 
             @pl.when(z == plane)

time: 83.3 us -> 78.8 us (0.946)
  Pallas kernels: 81.4 us -> 76.9 us
    pallas_call x1, Pallas kernels: 81.4 us -> 76.9 us  [local(): pl.pallas_call(kernel, name='layer', out_shape=jax.ShapeDtypeStruct((rows...]
where the time goes in v3:
time: 78.8 us; the launch traced here: 78.6 us
  Pallas kernels  76.9 us (98%)
  local copies, waits for them, and re-layouts  1.67 us (2%)
    pallas_call x1, Pallas kernels, local(): pl.pallas_call(kernel, name='layer', out_shape=jax.ShapeDtypeStruct((rows...  76.9 us
    unnamed x1, local copies, waits for them, and re-layouts  1.67 us

profile of v3, /device:TPU:1, one launch (start us, length us, event | category | flops | bytes accessed | tf_op | source)
XLA Modules:
  0.0 78.6 jit_solution(15287541257449148667)
XLA Ops:
  0.0 76.9 %layer.1 = bf16[128,1024]{1,0:T(8,128)(2,1)} custom-call(s32[8]{0:T(128)} %bitcast.3, bf16[128,1024]{1,0:T(8,128)(2,1)} %refs_1_.1, bf16[128,1024]{1,0:T(8,128)(2,1)} %refs_2_.1, bf16[128,1024]{1,0:T(8,128)(2,1)} %refs_3_.1, bf16[128,1024]{1,0:T(8,128)(2,1)} %refs_4_.1, f32[1,4096]{1,0:T(1,128)} %bitcast.2, bf16[1,4096,128]{2,1,0:T(8,128)(2,1)} %refs_6_.1, ...), custom_call_target="tpu_custom_call" | custom-call | tf_op jit(solution)/shard_map/layer/pallas_call | solution.py:974
  76.9 1.7 %copy.11 = bf16[128,1024]{1,0:T(8,128)(2,1)} copy(bf16[128,1024]{1,0:T(8,128)(2,1)} %layer.1) | data formatting | bytes 524288

commit v4 on v3

--- a/solution.py
+++ b/solution.py
@@ -222,6 +222,7 @@
         return len(lots) - 1
 
     final_lot = sent.shape[0] - 1
+    relay_lot = final_lot - 1
 
     def push(src, dst, recv_sem, device, lot=None):
         lot = lot_for(all_lots, src) if lot is None else lot
@@ -406,11 +407,11 @@
 
     taken = [set() for _ in range(PLANES)]
 
-    def made(here, plane, h):
+    def made(here, plane, h, hold=False):
         taken[here].add((plane, h))
         with mark(f"attend{plane}_{h}"):
             attend(here, plane, h)
-        if here < PLANES - 1:
+        if here < PLANES - 1 and not hold:
             send_line(here, 1, plane, h)
         if here > 0:
             send_line(here, -1, plane, h)
@@ -467,11 +468,12 @@
             pass_on(1, 1, 0, 1)
             home(2)
             pass_on(1, 1, 0, 2)
-            lower(2)
             pass_on(1, -1, 3, 1)
-        if step == 3:
+        if step == 2:
             pass_on(1, -1, 2, 3)
             pass_on(1, -1, 3, 3)
+        if step == 3:
+            lower(2)
         if step == 4:
             pass_on(1, -1, 3, 2)
 
@@ -487,11 +489,11 @@
             if h != STAY_HEAD:
                 send_part(2, -1, 1, h, yo)
 
-        def lower(h):
+        def lower(h, hold=False):
             with mark(f"lower{h}"):
                 got_above(h)
                 got_kv(below, h)
-            made(2, 3, h)
+            made(2, 3, h, hold)
 
         if step == 0:
             first(0)
@@ -505,25 +507,26 @@
             second(1)
             lower(0)
             second(3)
-            first(2)
             with mark("farther3"):
                 got_kv(farther, 3)
-            second(2)
             made(2, 2, 3)
             pass_on(2, 1, 1, 3)
             lower(1)
             pass_on(2, -1, 3, 3)
+            first(2)
+            second(2)
             pass_on(2, 1, 1, 0)
             pass_on(2, 1, 0, 3)
         if step == 1:
             pass_on(2, 1, 2, 0)
             pass_on(2, 1, 0, 0)
         if step == 2:
-            lower(2)
+            lower(2, True)
             pass_on(2, 1, 1, 1)
             pass_on(2, 1, 2, 1)
         if step == 3:
             pass_on(2, 1, 0, 1)
+            send_line(2, 1, 3, 2)
         if step == 4:
             pass_on(2, 1, 1, 2)
             pass_on(2, 1, 0, 2)
@@ -588,9 +591,10 @@
     def feature_at(pos, g):
         return pos + g.start
 
-    def feature(n, py, pt, pos, g, device, src=None):
+    def feature(n, py, pt, pos, g, device, src=None, lot=None):
         ref = x_buf.at[py, pt, heads_at[pos], g]
-        push(ref if src is None else src, ref, feat_r.at[lot_of[n], feature_at(pos, g)], device)
+        src = ref if src is None else src
+        push(src, ref, feat_r.at[lot_of[n], feature_at(pos, g)], device, lot)
 
     lot_of = (0, 0, 1, 2, 0, 3, 3)
     arrivals = (
@@ -636,11 +640,11 @@
             feature(4, y, t, pos, g, dev_yc, other)
             feature(0, y, t, pos, g, dev_c, other)
 
-    def second_stage(pos, g):
+    def second_stage(pos, g, lot=None):
         take(3, pos, g)
-        feature(5, yo, t, pos, g, dev_x)
+        feature(5, yo, t, pos, g, dev_x, lot=lot)
         take(2, pos, g)
-        feature(6, y, txc, pos, g, dev_y)
+        feature(6, y, txc, pos, g, dev_y, lot=lot)
 
     def near(pos, g):
         wait_for(3 * size_of(x_buf.at[y, t, 0, g]), feat_r.at[0, feature_at(pos, g)])
@@ -686,11 +690,21 @@
     gather(0)
     first_stage(0)
     planes(1)
+
+    @pl.when(z == 0)
+    def _():
+        with mark("second0"):
+            second_stage(0, both, relay_lot)
+
     gather(1)
     first_stage(1)
     planes(2)
-    with mark("second0"):
-        second_stage(0, both)
+
+    @pl.when(z > 0)
+    def _():
+        with mark("second0"):
+            second_stage(0, both, relay_lot)
+
     planes(3)
     gather(2)
     first_stage(2)
@@ -877,6 +891,7 @@
     with mark("drain"):
         for lot, amount in enumerate(all_lots):
             all_sent(sent.at[lot], amount)
+        all_sent(sent.at[relay_lot], 2 * size_of(x_buf.at[0, 0, 0]))
         all_sent(sent.at[final_lot], 3 * size_of(out_ref) // 4)
         for plane in range(PLANES):
 
@@ -963,7 +978,7 @@
         dma((chunks,)),
         dma((2, chunks)),
         dma((1,)),
-        dma((8,)),
+        dma((9,)),
         dma((4,)),
     )
     flat, tree = jax.tree.flatten(scratch, is_leaf=lambda leaf: not isinstance(leaf, (list, tuple)))
@@ -974,7 +989,7 @@
     return pl.pallas_call(
         kernel,
         name="layer",
-        out_shape=jax.ShapeDtypeStruct((rows, width), BF16),
+        out_shape=pltpu.VMEM((rows, width), BF16),
         in_specs=[pl.BlockSpec(memory_space=pltpu.SMEM)]
         + [anywhere] * 4
         + [vmem]
@@ -982,7 +997,7 @@
         out_specs=vmem,
         scratch_shapes=flat,
         compiler_params=pltpu.CompilerParams(
-            collective_id=0, has_side_effects=True, vmem_limit_bytes=67043328
+            collective_id=0, has_side_effects=True, vmem_limit_bytes=67043328 - 2 * rows * width
         ),
     )(
         routing.reshape(-1),

time: 78.8 us -> 76.8 us (0.975)
  Pallas kernels: 76.9 us -> 75.8 us
  local copies, waits for them, and re-layouts: 1.67 us -> 0.71 us
    pallas_call x1, Pallas kernels: 76.9 us -> 75.8 us  [local(): pl.pallas_call(kernel, name='layer', out_shape=pltpu.VMEM((rows, width),...]
    unnamed x1, local copies, waits for them, and re-layouts: 1.67 us -> 0.71 us
where the time goes in v4:
time: 76.8 us; the launch traced here: 76.5 us
  Pallas kernels  75.8 us (99%)
    pallas_call x1, Pallas kernels, local(): pl.pallas_call(kernel, name='layer', out_shape=pltpu.VMEM((rows, width),...  75.8 us

profile of v4, /device:TPU:1, one launch (start us, length us, event | category | flops | bytes accessed | tf_op | source)
XLA Modules:
  0.0 76.5 jit_solution(7688328887160318915)
XLA Ops:
  0.0 75.8 %layer.1 = bf16[128,1024]{1,0:T(8,128)(2,1)S(1)} custom-call(s32[8]{0:T(128)} %bitcast.3, bf16[128,1024]{1,0:T(8,128)(2,1)} %refs_1_.1, bf16[128,1024]{1,0:T(8,128)(2,1)} %refs_2_.1, bf16[128,1024]{1,0:T(8,128)(2,1)} %refs_3_.1, bf16[128,1024]{1,0:T(8,128)(2,1)} %refs_4_.1, f32[1,4096]{1,0:T(1,128)} %bitcast.2, bf16[1,4096,128]{2,1,0:T(8,128)(2,1)} %refs_6_.1, ...), custom_call_target="tpu_custom_call" | custom-call | tf_op jit(solution)/shard_map/layer/pallas_call | solution.py:989
  75.8 0.7 copy.11

commit v5 on v4

--- a/solution.py
+++ b/solution.py
@@ -123,8 +123,8 @@
 BF16 = jnp.bfloat16
 F32 = jnp.float32
 PLANES = 4
-GROUPS = 2
-SPAN = HEAD_DIM
+GROUPS = 4
+SPAN = 2 * HEAD_DIM
 STAY_HEAD = 3
 
 
@@ -455,8 +455,8 @@
             first(3)
             first(0)
             home(3)
+            first(1)
             home(0)
-            first(1)
             lower(0)
             pass_on(1, 1, 0, 3)
             pass_on(1, 1, 0, 0)
@@ -498,13 +498,13 @@
         if step == 0:
             first(0)
             second(0)
-            send_home(2, -1, 2, (0, 1))
             first(3)
             first(1)
             with mark("below3"):
                 got_kv(below, 3)
             send_kv(2, 1, below, farther, 3)
             second(1)
+            send_home(2, -1, 2, (0, 1))
             lower(0)
             second(3)
             with mark("farther3"):
@@ -539,7 +539,7 @@
                     own(kind, h)
                 if h != STAY_HEAD:
                     send_part(3, -1, kind, h, yo)
-                    if (kind, h) == (1, 0):
+                    if (kind, h) == (1, 1):
                         send_home(3, -1, 2, (0, 1))
                 elif kind == 1:
                     with mark("below3"):
@@ -594,9 +594,11 @@
     def feature(n, py, pt, pos, g, device, src=None, lot=None):
         ref = x_buf.at[py, pt, heads_at[pos], g]
         src = ref if src is None else src
-        push(src, ref, feat_r.at[lot_of[n], feature_at(pos, g)], device, lot)
-
-    lot_of = (0, 0, 1, 2, 0, 3, 3)
+        push(src, ref, feat_r.at[lot_of(n, pos), feature_at(pos, g)], device, lot)
+
+    def lot_of(n, pos):
+        return ((0, 2, 1, 0, 0, 3, 3) if pos == ends else (0, 0, 1, 2, 0, 3, 3))[n]
+
     arrivals = (
         (y, tc),
         (y, tx),
@@ -609,7 +611,7 @@
 
     def take(n, pos, g):
         py, pt = arrivals[n]
-        got(x_buf.at[py, pt, heads_at[pos], g], feat_r.at[lot_of[n], feature_at(pos, g)])
+        got(x_buf.at[py, pt, heads_at[pos], g], feat_r.at[lot_of(n, pos), feature_at(pos, g)])
 
     def choose(h, g):
         for r in range(most):
@@ -641,8 +643,12 @@
             feature(0, y, t, pos, g, dev_c, other)
 
     def second_stage(pos, g, lot=None):
-        take(3, pos, g)
-        feature(5, yo, t, pos, g, dev_x, lot=lot)
+        if pos == ends:
+            take(1, pos, g)
+            feature(5, y, tx, pos, g, dev_y, lot=lot)
+        else:
+            take(3, pos, g)
+            feature(5, yo, t, pos, g, dev_x, lot=lot)
         take(2, pos, g)
         feature(6, y, txc, pos, g, dev_y, lot=lot)
 
@@ -675,7 +681,7 @@
 
     every_part = [(y, t)] + list(arrivals)
 
-    g0, g1 = groups_of(ends)
+    parts_last = groups_of(ends)
     both = groups_of(0)[0]
     planes(0)
     weights = (
@@ -712,10 +718,10 @@
         second_stage(1, both)
     planes(4)
     gather(3)
-    first_stage(3, [g0])
+    first_stage(3, parts_last[:1])
     with mark("second2"):
         second_stage(2, both)
-    first_stage(3, [g1])
+    first_stage(3, parts_last[1:])
     acc_buf[...] = jnp.zeros_like(acc_buf)
     square_buf[...] = jnp.zeros_like(square_buf)
     with mark("weights"):
@@ -730,27 +736,32 @@
         with mark(f"expert{pos}"):
             expert_parts(every_part, pos, both)
 
-    whole(0)
-    with mark("secondL0"):
-        second_stage(ends, g0)
-    with mark("secondL1"):
-        second_stage(ends, g1)
-    whole(1)
-    whole(2)
-    for g in (g0, g1):
-        with mark(f"nearL{g.start}"):
+    def relay_last(g):
+        with mark(f"secondL{g.start}"):
+            second_stage(ends, g)
+
+    def hide(g):
+        i = g.start
+        with mark(f"nearL{i}"):
             near(ends, g)
-        with mark(f"farL{g.start}"):
+        with mark(f"farL{i}"):
             far(ends, g)
-        with mark(f"expertL{g.start}"):
+        with mark(f"expertL{i}"):
             expert_parts(every_part, ends, g)
-            i = g.start
             scale = lax.rsqrt(square_buf[i] * (1.0 / features) + epsilon)
             gate_val = acc_buf[i, :, pl.ds(0, 2 * units)] * scale
             up_val = acc_buf[i, :, pl.ds(2 * units, 2 * units)] * scale
             hid_buf[x, i] = (gate_val / (1.0 + jnp.exp(-gate_val)) * up_val).astype(BF16)
         push(hid_buf.at[x, i], hid_buf.at[x, i], hid_r.at[i], dev_x)
 
+    whole(0)
+    relay_last(parts_last[0])
+    whole(1)
+    relay_last(parts_last[1])
+    whole(2)
+    for g in parts_last[2:]:
+        relay_last(g)
+
     wide = half // SPAN
     pieces = [(s, j) for s in range(2) for j in range(wide)]
 
@@ -758,6 +769,7 @@
         return (i * 2 + s) * wide + j
 
     pair = 2 * SPAN
+    per = SPAN // HEAD_DIM
 
     def branch(i, s, which, j):
         hidden = jnp.concatenate([hid_buf[n, i] for n in range(2)], axis=1)
@@ -777,7 +789,13 @@
                     push(b_out.at[k], b_in.at[k], branch_r.at[k], dev_y)
             for s, j in doubles:
                 for m, (k, value) in enumerate(branch(i, s, y, j)):
-                    stream = x_buf[y, t if s == 0 else tc, 2 * j + m, i]
+                    stream = jnp.concatenate(
+                        [
+                            x_buf[y, t if s == 0 else tc, (2 * j + m) * per + q, i]
+                            for q in range(per)
+                        ],
+                        axis=1,
+                    )
                     part[k] = stream.astype(F32) + value.astype(F32)
 
     def blend(i, s, j):
@@ -873,10 +891,22 @@
         arrive(i, s, j, 2)
 
     every = [(i, s, j) for i in range(GROUPS) for s, j in pieces]
-    for i in range(GROUPS):
-        down(i)
-    stages = ((0, blend), (4, turn_in), (9, carry), (12, arrive_middle), (16, arrive_end))
+    for g in parts_last[:3]:
+        hide(g)
+    down(0)
+    hide(parts_last[3])
+    down(1)
+    down(2)
+    stages = (
+        (0, blend),
+        (4, turn_in),
+        (9, carry),
+        (12, arrive_middle),
+        (16, arrive_end),
+    )
     for n in range(len(every) + stages[-1][0]):
+        if n == len(pieces):
+            down(3)
         for lag, stage in stages:
             if 0 <= n - lag < len(every):
                 stage(*every[n - lag])

time: 76.8 us -> 76 us (0.990)
  Pallas kernels: 75.8 us -> 75 us
    pallas_call x1, Pallas kernels: 75.8 us -> 75 us  [local(): pl.pallas_call(kernel, name='layer', out_shape=pltpu.VMEM((rows, width),...]
where the time goes in v5:
time: 76 us; the launch traced here: 75.7 us
  Pallas kernels  75 us (99%)
    pallas_call x1, Pallas kernels, local(): pl.pallas_call(kernel, name='layer', out_shape=pltpu.VMEM((rows, width),...  75 us

profile of v5, /device:TPU:1, one launch (start us, length us, event | category | flops | bytes accessed | tf_op | source)
XLA Modules:
  0.0 75.7 jit_solution(8937458910056513643)
XLA Ops:
  0.0 75.0 %layer.1 = bf16[128,1024]{1,0:T(8,128)(2,1)S(1)} custom-call(s32[8]{0:T(128)} %bitcast.3, bf16[128,1024]{1,0:T(8,128)(2,1)} %refs_1_.1, bf16[128,1024]{1,0:T(8,128)(2,1)} %refs_2_.1, bf16[128,1024]{1,0:T(8,128)(2,1)} %refs_3_.1, bf16[128,1024]{1,0:T(8,128)(2,1)} %refs_4_.1, f32[1,4096]{1,0:T(1,128)} %bitcast.2, bf16[1,4096,128]{2,1,0:T(8,128)(2,1)} %refs_6_.1, ...), custom_call_target="tpu_custom_call" | custom-call | tf_op jit(solution)/shard_map/layer/pallas_call | solution.py:1019
  75.0 0.7 copy.11

commit v6 on v5

--- a/solution.py
+++ b/solution.py
@@ -208,6 +208,7 @@
     dev_y, dev_yc = (mate, t), (mate, tc)
     dev_x, dev_xc = (me, tx), (me, txc)
     dev_c = (me, tc)
+    dev_d, dev_dc = (mate, tx), (mate, txc)
     dev_up, dev_dn = (me + 2, t), (me - 2, t)
     has_up, has_dn = z < PLANES - 1, z > 0
 
@@ -597,7 +598,7 @@
         push(src, ref, feat_r.at[lot_of(n, pos), feature_at(pos, g)], device, lot)
 
     def lot_of(n, pos):
-        return ((0, 2, 1, 0, 0, 3, 3) if pos == ends else (0, 0, 1, 2, 0, 3, 3))[n]
+        return 0 if pos == ends else (0, 0, 1, 2, 0, 3, 3)[n]
 
     arrivals = (
         (y, tc),
@@ -641,14 +642,13 @@
             feature(1, y, t, pos, g, dev_x)
             feature(4, y, t, pos, g, dev_yc, other)
             feature(0, y, t, pos, g, dev_c, other)
+            if pos == ends:
+                feature(5, y, t, pos, g, dev_d)
+                feature(6, y, t, pos, g, dev_dc, other)
 
     def second_stage(pos, g, lot=None):
-        if pos == ends:
-            take(1, pos, g)
-            feature(5, y, tx, pos, g, dev_y, lot=lot)
-        else:
-            take(3, pos, g)
-            feature(5, yo, t, pos, g, dev_x, lot=lot)
+        take(3, pos, g)
+        feature(5, yo, t, pos, g, dev_x, lot=lot)
         take(2, pos, g)
         feature(6, y, txc, pos, g, dev_y, lot=lot)
 
@@ -736,16 +736,10 @@
         with mark(f"expert{pos}"):
             expert_parts(every_part, pos, both)
 
-    def relay_last(g):
-        with mark(f"secondL{g.start}"):
-            second_stage(ends, g)
-
     def hide(g):
         i = g.start
-        with mark(f"nearL{i}"):
-            near(ends, g)
         with mark(f"farL{i}"):
-            far(ends, g)
+            wait_for(7 * size_of(x_buf.at[y, t, 0, g]), feat_r.at[0, feature_at(ends, g)])
         with mark(f"expertL{i}"):
             expert_parts(every_part, ends, g)
             scale = lax.rsqrt(square_buf[i] * (1.0 / features) + epsilon)
@@ -754,13 +748,8 @@
             hid_buf[x, i] = (gate_val / (1.0 + jnp.exp(-gate_val)) * up_val).astype(BF16)
         push(hid_buf.at[x, i], hid_buf.at[x, i], hid_r.at[i], dev_x)
 
-    whole(0)
-    relay_last(parts_last[0])
-    whole(1)
-    relay_last(parts_last[1])
-    whole(2)
-    for g in parts_last[2:]:
-        relay_last(g)
+    for pos in range(ends):
+        whole(pos)
 
     wide = half // SPAN
     pieces = [(s, j) for s in range(2) for j in range(wide)]

time: 76 us -> 76.1 us (level)
  no operation moved by 1% of the time
where the time goes in v6:
time: 76.1 us; the launch traced here: 75.9 us
  Pallas kernels  75.2 us (99%)
    pallas_call x1, Pallas kernels, local(): pl.pallas_call(kernel, name='layer', out_shape=pltpu.VMEM((rows, width),...  75.2 us

profile of v6, /device:TPU:1, one launch (start us, length us, event | category | flops | bytes accessed | tf_op | source)
XLA Modules:
  0.0 75.9 jit_solution(14012304111422259145)
XLA Ops:
  0.0 75.2 %layer.1 = bf16[128,1024]{1,0:T(8,128)(2,1)S(1)} custom-call(s32[8]{0:T(128)} %bitcast.3, bf16[128,1024]{1,0:T(8,128)(2,1)} %refs_1_.1, bf16[128,1024]{1,0:T(8,128)(2,1)} %refs_2_.1, bf16[128,1024]{1,0:T(8,128)(2,1)} %refs_3_.1, bf16[128,1024]{1,0:T(8,128)(2,1)} %refs_4_.1, f32[1,4096]{1,0:T(1,128)} %bitcast.2, bf16[1,4096,128]{2,1,0:T(8,128)(2,1)} %refs_6_.1, ...), custom_call_target="tpu_custom_call" | custom-call | tf_op jit(solution)/shard_map/layer/pallas_call | solution.py:1008
  75.2 0.7 copy.11

commit v7 on v5

--- a/solution.py
+++ b/solution.py
@@ -171,6 +171,8 @@
         dn_out,
         dn_in,
         fin,
+        home_in,
+        far_in,
         own_s,
         away_s,
         weight_s,
@@ -184,6 +186,8 @@
         end_r,
         ret_r,
         last_r,
+        home_r,
+        far_r,
         sent,
         plane_sent,
     ) = scratch
@@ -221,8 +225,7 @@
         lots[-1] += size_of(ref)
         return len(lots) - 1
 
-    final_lot = sent.shape[0] - 1
-    relay_lot = final_lot - 1
+    relay_lot = sent.shape[0] - 1
 
     def push(src, dst, recv_sem, device, lot=None):
         lot = lot_for(all_lots, src) if lot is None else lot
@@ -594,11 +597,9 @@
     def feature(n, py, pt, pos, g, device, src=None, lot=None):
         ref = x_buf.at[py, pt, heads_at[pos], g]
         src = ref if src is None else src
-        push(src, ref, feat_r.at[lot_of(n, pos), feature_at(pos, g)], device, lot)
-
-    def lot_of(n, pos):
-        return ((0, 2, 1, 0, 0, 3, 3) if pos == ends else (0, 0, 1, 2, 0, 3, 3))[n]
-
+        push(src, ref, feat_r.at[lot_of[n], feature_at(pos, g)], device, lot)
+
+    lot_of = (0, 0, 1, 2, 0, 3, 3)
     arrivals = (
         (y, tc),
         (y, tx),
@@ -611,7 +612,7 @@
 
     def take(n, pos, g):
         py, pt = arrivals[n]
-        got(x_buf.at[py, pt, heads_at[pos], g], feat_r.at[lot_of(n, pos), feature_at(pos, g)])
+        got(x_buf.at[py, pt, heads_at[pos], g], feat_r.at[lot_of[n], feature_at(pos, g)])
 
     def choose(h, g):
         for r in range(most):
@@ -643,12 +644,8 @@
             feature(0, y, t, pos, g, dev_c, other)
 
     def second_stage(pos, g, lot=None):
-        if pos == ends:
-            take(1, pos, g)
-            feature(5, y, tx, pos, g, dev_y, lot=lot)
-        else:
-            take(3, pos, g)
-            feature(5, yo, t, pos, g, dev_x, lot=lot)
+        take(3, pos, g)
+        feature(5, yo, t, pos, g, dev_x, lot=lot)
         take(2, pos, g)
         feature(6, y, txc, pos, g, dev_y, lot=lot)
 
@@ -840,13 +837,53 @@
 
     def carry(i, s, j):
         k = chunk(i, s, j)
-        for here, way, d, arrived in ((2, 0, 3, up_in), (1, 1, 0, dn_in)):
+        for here, way, d, out, arrived in ((2, 0, 3, up_out, up_in), (1, 1, 0, dn_out, dn_in)):
 
             @pl.when(z == here)
             def _():
                 with mark(f"carry{k}"):
                     got(arrived.at[k, d], ret_r.at[d % 2, k])
-                give(here, way, k, d, lambda b, n: arrived[k, d, n])
+                for n in range(2):
+                    b = 2 * d + n
+                    out[k, d, n] = pick(expert[b] == here, mix[k][slot[b]], arrived[k, d, n])
+                    push_plane(
+                        here,
+                        out.at[k, d, n],
+                        far_in.at[y, c, i, j],
+                        far_r.at[i * wide + j],
+                        (b, t if s == 0 else tc),
+                    )
+
+    def settle(i, s, j):
+        k = chunk(i, s, j)
+        for d in (0, PLANES - 1):
+
+            @pl.when(z == d)
+            def _():
+                for n, which in enumerate((y, yo)):
+                    at = slot[2 * d] + which * (slot[2 * d + 1] - slot[2 * d])
+                    fin[k, n] = mix[k][at]
+                there = home_in.at[y, c, i, j]
+                sem = home_r.at[i * wide + j]
+                push_plane(d, fin.at[k, 1], there, sem, dev_y if s == 0 else dev_yc)
+                if s == 0:
+                    there[...] = fin[k, 0]
+                else:
+                    push_plane(d, fin.at[k, 0], there, sem, dev_c)
+
+    def final(i, j):
+        for d in (0, PLANES - 1):
+
+            @pl.when(z == d)
+            def _():
+                with mark(f"final{i}_{j}"):
+                    wait_for(3 * size_of(fin.at[0, 0]), home_r.at[i * wide + j])
+                    wait_for(4 * size_of(fin.at[0, 0]), far_r.at[i * wide + j])
+                flag = jnp.where(y == 0, expert[2 * d], expert[2 * d + 1]) == d
+                for half_at in range(2):
+                    for side in range(2):
+                        at = (half_at, side, i, j)
+                        target(side, i, half_at, j)[...] = pick(flag, home_in[at], far_in[at])
 
     def target(side, i, which, j):
         return out_ref.at[
@@ -860,31 +897,20 @@
         @pl.when(z == d)
         def _():
             with mark(f"arrive{k}"):
-                if d > 1:
-                    got(up_in.at[k, d], ret_r.at[d % 2, k])
-                if d < PLANES - 2:
-                    got(dn_in.at[k, d], ret_r.at[d % 2, k])
+                got((up_in if d > 1 else dn_in).at[k, d], ret_r.at[d % 2, k])
             for n in range(2):
                 b = 2 * d + n
-                value = mix[k][slot[b]]
-                if d > 0:
-                    lower = up_in[k, d, n] if d > 1 else end_in[k][slot[b]]
-                    value = pick(expert[b] < d, lower, value)
-                if d < PLANES - 1:
-                    higher = dn_in[k, d, n] if d < PLANES - 2 else end_in[k][slot[b]]
-                    value = pick(expert[b] > d, higher, value)
-                fin[k, n] = value
+                lower = up_in[k, d, n] if d > 1 else end_in[k][slot[b]]
+                higher = dn_in[k, d, n] if d == 1 else end_in[k][slot[b]]
+                value = pick(expert[b] < d, lower, mix[k][slot[b]])
+                fin[k, n] = pick(expert[b] > d, higher, value)
             mine = target(c, i, y, j)
             device = dev_y if s == 0 else dev_yc
-            push(fin.at[k, yo], mine, last_r.at[0], device, final_lot)
+            push_plane(d, fin.at[k, yo], mine, last_r.at[0], device)
             if s == 0:
                 mine[...] = fin[k, y]
             else:
-                push(fin.at[k, y], mine, last_r.at[0], dev_c, final_lot)
-
-    def arrive_end(i, s, j):
-        arrive(i, s, j, 0)
-        arrive(i, s, j, PLANES - 1)
+                push_plane(d, fin.at[k, y], mine, last_r.at[0], dev_c)
 
     def arrive_middle(i, s, j):
         arrive(i, s, j, 1)
@@ -902,7 +928,7 @@
         (4, turn_in),
         (9, carry),
         (12, arrive_middle),
-        (16, arrive_end),
+        (16, settle),
     )
     for n in range(len(every) + stages[-1][0]):
         if n == len(pieces):
@@ -911,7 +937,13 @@
             if 0 <= n - lag < len(every):
                 stage(*every[n - lag])
     with mark("lastwait"):
-        wait_for(3 * size_of(out_ref) // 4, last_r.at[0])
+        for i in range(GROUPS):
+            for j in range(wide):
+                final(i, j)
+
+        @pl.when((z > 0) & (z < PLANES - 1))
+        def _():
+            wait_for(3 * size_of(out_ref) // 4, last_r.at[0])
 
     def all_sent(sem, amount):
         if amount:
@@ -922,7 +954,6 @@
         for lot, amount in enumerate(all_lots):
             all_sent(sent.at[lot], amount)
         all_sent(sent.at[relay_lot], 2 * size_of(x_buf.at[0, 0, 0]))
-        all_sent(sent.at[final_lot], 3 * size_of(out_ref) // 4)
         for plane in range(PLANES):
 
             @pl.when(z == plane)
@@ -995,6 +1026,8 @@
         room(chunks, planes, 2, group_rows, SPAN),
         room(chunks, planes, 2, group_rows, SPAN),
         room(chunks, 2, group_rows, SPAN),
+        room(2, 2, GROUPS, wide, group_rows, SPAN),
+        room(2, 2, GROUPS, wide, group_rows, SPAN),
         dma((1,)),
         dma((1,)),
         dma((1,)),
@@ -1008,7 +1041,9 @@
         dma((chunks,)),
         dma((2, chunks)),
         dma((1,)),
-        dma((9,)),
+        dma((GROUPS * wide,)),
+        dma((GROUPS * wide,)),
+        dma((8,)),
         dma((4,)),
     )
     flat, tree = jax.tree.flatten(scratch, is_leaf=lambda leaf: not isinstance(leaf, (list, tuple)))

time: 76 us -> 74.2 us (0.976)
  Pallas kernels: 75 us -> 73.2 us
    pallas_call x1, Pallas kernels: 75 us -> 73.2 us  [local(): pl.pallas_call(kernel, name='layer', out_shape=pltpu.VMEM((rows, width),...]
where the time goes in v7:
time: 74.2 us; the launch traced here: 74 us
  Pallas kernels  73.2 us (99%)
    pallas_call x1, Pallas kernels, local(): pl.pallas_call(kernel, name='layer', out_shape=pltpu.VMEM((rows, width),...  73.2 us

profile of v7, /device:TPU:1, one launch (start us, length us, event | category | flops | bytes accessed | tf_op | source)
XLA Modules:
  0.0 74.0 jit_solution(1246267613100715928)
XLA Ops:
  0.0 73.2 %layer.1 = bf16[128,1024]{1,0:T(8,128)(2,1)S(1)} custom-call(s32[8]{0:T(128)} %bitcast.3, bf16[128,1024]{1,0:T(8,128)(2,1)} %refs_1_.1, bf16[128,1024]{1,0:T(8,128)(2,1)} %refs_2_.1, bf16[128,1024]{1,0:T(8,128)(2,1)} %refs_3_.1, bf16[128,1024]{1,0:T(8,128)(2,1)} %refs_4_.1, f32[1,4096]{1,0:T(1,128)} %bitcast.2, bf16[1,4096,128]{2,1,0:T(8,128)(2,1)} %refs_6_.1, ...), custom_call_target="tpu_custom_call" | custom-call | tf_op jit(solution)/shard_map/layer/pallas_call | solution.py:1054
  73.2 0.7 copy.11

commit v8 on v7

--- a/solution.py
+++ b/solution.py
@@ -333,7 +333,7 @@
     col_at = lax.broadcasted_iota(jnp.int32, (rows, rows), 1)
     below, above, farther = 1, 2, 3
 
-    def attend(here, plane, h):
+    def attend(here, plane, h, ways):
         side = 0 if plane == here else 1
         keep = {here: 0, here - 1: below, here + 1: above, here - 2: farther}
         reach = WINDOW // rows
@@ -374,6 +374,9 @@
             )
             stream = (qr_buf[side, h, 1, n].astype(F32) + attended).astype(BF16)
             line[h][block] = stream.reshape(2, core_rows, HEAD_DIM)
+            for way in ways:
+                ref = line[h].at[block]
+                push_plane(here, ref, ref, line_r.at[plane, h], device_at(way))
 
     def device_at(way):
         return dev_up if way > 0 else dev_dn
@@ -412,12 +415,13 @@
 
     def made(here, plane, h, hold=False):
         taken[here].add((plane, h))
+        ways = []
+        if here < PLANES - 1 and not hold:
+            ways.append(1)
+        if here > 0:
+            ways.append(-1)
         with mark(f"attend{plane}_{h}"):
-            attend(here, plane, h)
-        if here < PLANES - 1 and not hold:
-            send_line(here, 1, plane, h)
-        if here > 0:
-            send_line(here, -1, plane, h)
+            attend(here, plane, h, ways)
 
     def pass_on(here, way, plane, h):
         with mark(f"pass{plane}_{h}"):
@@ -599,7 +603,7 @@
         src = ref if src is None else src
         push(src, ref, feat_r.at[lot_of[n], feature_at(pos, g)], device, lot)
 
-    lot_of = (0, 0, 1, 2, 0, 3, 3)
+    lot_of = (0, 0, 1, 2, 0, 0, 0)
     arrivals = (
         (y, tc),
         (y, tx),
@@ -649,11 +653,8 @@
         take(2, pos, g)
         feature(6, y, txc, pos, g, dev_y, lot=lot)
 
-    def near(pos, g):
-        wait_for(3 * size_of(x_buf.at[y, t, 0, g]), feat_r.at[0, feature_at(pos, g)])
-
-    def far(pos, g):
-        wait_for(2 * size_of(x_buf.at[y, t, 0, g]), feat_r.at[3, feature_at(pos, g)])
+    def complete(pos, g):
+        wait_for(5 * size_of(x_buf.at[y, t, 0, g]), feat_r.at[0, feature_at(pos, g)])
 
     def expert_parts(parts, pos, g):
         depth = g.size * most * group_rows
@@ -728,8 +729,7 @@
 
     def whole(pos):
         with mark(f"feat{pos}"):
-            near(pos, both)
-            far(pos, both)
+            complete(pos, both)
         with mark(f"expert{pos}"):
             expert_parts(every_part, pos, both)
 
@@ -739,10 +739,8 @@
 
     def hide(g):
         i = g.start
-        with mark(f"nearL{i}"):
-            near(ends, g)
         with mark(f"farL{i}"):
-            far(ends, g)
+            complete(ends, g)
         with mark(f"expertL{i}"):
             expert_parts(every_part, ends, g)
             scale = lax.rsqrt(square_buf[i] * (1.0 / features) + epsilon)
@@ -864,7 +862,7 @@
                     at = slot[2 * d] + which * (slot[2 * d + 1] - slot[2 * d])
                     fin[k, n] = mix[k][at]
                 there = home_in.at[y, c, i, j]
-                sem = home_r.at[i * wide + j]
+                sem = home_r.at[0]
                 push_plane(d, fin.at[k, 1], there, sem, dev_y if s == 0 else dev_yc)
                 if s == 0:
                     there[...] = fin[k, 0]
@@ -877,7 +875,8 @@
             @pl.when(z == d)
             def _():
                 with mark(f"final{i}_{j}"):
-                    wait_for(3 * size_of(fin.at[0, 0]), home_r.at[i * wide + j])
+                    if i == 0 and j == 0:
+                        wait_for(3 * GROUPS * wide * size_of(fin.at[0, 0]), home_r.at[0])
                     wait_for(4 * size_of(fin.at[0, 0]), far_r.at[i * wide + j])
                 flag = jnp.where(y == 0, expert[2 * d], expert[2 * d + 1]) == d
                 for half_at in range(2):
@@ -1034,14 +1033,14 @@
         dma((2, heads)),
         dma((2 * heads + 1,)),
         dma((planes, heads)),
-        dma((4, heads + GROUPS - 1)),
+        dma((3, heads + GROUPS - 1)),
         dma((1,)),
         dma((GROUPS,)),
         dma((chunks,)),
         dma((chunks,)),
         dma((2, chunks)),
         dma((1,)),
-        dma((GROUPS * wide,)),
+        dma((1,)),
         dma((GROUPS * wide,)),
         dma((8,)),
         dma((4,)),

time: 74.2 us -> 73.5 us (level)
  no operation moved by 1% of the time
where the time goes in v8:
time: 73.5 us; the launch traced here: 73.2 us
  Pallas kernels  72.5 us (99%)
    pallas_call x1, Pallas kernels, local(): pl.pallas_call(kernel, name='layer', out_shape=pltpu.VMEM((rows, width),...  72.5 us

profile of v8, /device:TPU:1, one launch (start us, length us, event | category | flops | bytes accessed | tf_op | source)
XLA Modules:
  0.0 73.2 jit_solution(15534505823427745799)
XLA Ops:
  0.0 72.5 %layer.1 = bf16[128,1024]{1,0:T(8,128)(2,1)S(1)} custom-call(s32[8]{0:T(128)} %bitcast.3, bf16[128,1024]{1,0:T(8,128)(2,1)} %refs_1_.1, bf16[128,1024]{1,0:T(8,128)(2,1)} %refs_2_.1, bf16[128,1024]{1,0:T(8,128)(2,1)} %refs_3_.1, bf16[128,1024]{1,0:T(8,128)(2,1)} %refs_4_.1, f32[1,4096]{1,0:T(1,128)} %bitcast.2, bf16[1,4096,128]{2,1,0:T(8,128)(2,1)} %refs_6_.1, ...), custom_call_target="tpu_custom_call" | custom-call | tf_op jit(solution)/shard_map/layer/pallas_call | solution.py:1053
  72.5 0.7 copy.11

commit v9 on v8

--- a/solution.py
+++ b/solution.py
@@ -215,7 +215,7 @@
     dev_up, dev_dn = (me + 2, t), (me - 2, t)
     has_up, has_dn = z < PLANES - 1, z > 0
 
-    limit = size_of(w_buf.at[0])
+    limit = size_of(w_buf)
     all_lots = [0]
     plane_lots = [[0] for _ in range(PLANES)]
 
@@ -946,7 +946,7 @@
 
     def all_sent(sem, amount):
         if amount:
-            ref = w_buf.at[0, pl.ds(0, amount // (2 * units))]
+            ref = w_buf.at[:, pl.ds(0, amount // (8 * units))]
             remote(ref, ref, sem, hid_r.at[0], dev_y).wait_send()
 
     with mark("drain"):
@@ -1042,8 +1042,8 @@
         dma((1,)),
         dma((1,)),
         dma((GROUPS * wide,)),
-        dma((8,)),
-        dma((4,)),
+        dma((3,)),
+        dma((1,)),
     )
     flat, tree = jax.tree.flatten(scratch, is_leaf=lambda leaf: not isinstance(leaf, (list, tuple)))
 

time: 73.5 us -> 73.4 us (level)
  no operation moved by 1% of the time
where the time goes in v9:
time: 73.4 us; the launch traced here: 73.1 us
  Pallas kernels  72.4 us (99%)
    pallas_call x1, Pallas kernels, local(): pl.pallas_call(kernel, name='layer', out_shape=pltpu.VMEM((rows, width),...  72.4 us

profile of v9, /device:TPU:1, one launch (start us, length us, event | category | flops | bytes accessed | tf_op | source)
XLA Modules:
  0.0 73.1 jit_solution(16836953944872070751)
XLA Ops:
  0.0 72.4 %layer.1 = bf16[128,1024]{1,0:T(8,128)(2,1)S(1)} custom-call(s32[8]{0:T(128)} %bitcast.3, bf16[128,1024]{1,0:T(8,128)(2,1)} %refs_1_.1, bf16[128,1024]{1,0:T(8,128)(2,1)} %refs_2_.1, bf16[128,1024]{1,0:T(8,128)(2,1)} %refs_3_.1, bf16[128,1024]{1,0:T(8,128)(2,1)} %refs_4_.1, f32[1,4096]{1,0:T(1,128)} %bitcast.2, bf16[1,4096,128]{2,1,0:T(8,128)(2,1)} %refs_6_.1, ...), custom_call_target="tpu_custom_call" | custom-call | tf_op jit(solution)/shard_map/layer/pallas_call | solution.py:1053
  72.4 0.7 copy.11
